TPU v7x, 32 devices: a whole 2x2x4 slice. The times are simulated.
32 devices in a mesh: tm: 2 (over x), sx: 4 (over z), sy: 4 (over y, core).
Axes of the slice: x: 2, y: 2, z: 4, core: 2. Of those that a mesh axis runs over, the one named last changes fastest.
Arguments:
- heat_source: float32 [8, 64, 64, 128], P('tm', 'sx', 'sy'), may hold values from -8 to 8
- conductivity: float32 [64, 64, 128], P('sx', 'sy'), may hold values from 0.001 to 0.5
- initial_iterate: float32 [8, 64, 64, 128], P('tm', 'sx', 'sy'), may hold values from -6 to 6
Outputs:
- solution: float32 [8, 64, 64, 128], P('tm', 'sx', 'sy')
- residual: float32 [8, 64, 64, 128], P('tm', 'sx', 'sy')
All inputs are finite; a program needn't handle non-finite values.
Results may differ from a plain program's by a relative error of at most 0.000074.
Values sent between devices are 32-bit elements; how exact they have to be, the bound alone decides.
A program may use at most 64 MiB of HBM per device.

v0:
```python
import jax
import jax.numpy as jnp
from jax import lax
from jax.sharding import PartitionSpec as P

relax_weight = 0.8
fine_step = 1.0


def padded_2(cells, sides, width):
    for axis, dim in sides:
        count = lax.axis_size(axis)
        ends = count - 1
        head = lax.slice_in_dim(cells, 0, width, axis=dim)
        tail = lax.slice_in_dim(cells, cells.shape[dim] - width, cells.shape[dim], axis=dim)
        cells = jnp.concatenate(
            [
                lax.ppermute(tail, axis, [(i, (i + 1) % count) for i in range(ends)]),
                cells,
                lax.ppermute(head, axis, [((i + 1) % count, i) for i in range(ends)]),
            ],
            axis=dim,
        )
    return cells


def shifted(value, axis, by):
    devices = lax.axis_size(axis)
    pairs = [(i, i + by) for i in range(devices) if 0 <= i + by < devices]
    return lax.ppermute(value, axis, pairs)


def partner_2(value, axis, stride):
    return lax.ppermute(value, axis, [(i, i ^ 1 << stride) for i in range(lax.axis_size(axis))])


def face_terms(conductivity):
    bordered = padded_2(conductivity, (("sx", 0), ("sy", 1)), 1)
    padded = jnp.pad(bordered, ((0, 0), (0, 0), (1, 1)))
    couple = (
        0.5 * (conductivity + padded[2:, 1:-1, 1:-1]),
        0.5 * (conductivity + padded[:-2, 1:-1, 1:-1]),
        0.5 * (conductivity + padded[1:-1, 2:, 1:-1]),
        0.5 * (conductivity + padded[1:-1, :-2, 1:-1]),
        0.5 * (conductivity + padded[1:-1, 1:-1, 2:]),
        0.5 * (conductivity + padded[1:-1, 1:-1, :-2]),
    )
    coupling = couple[0] + couple[1] + couple[2] + couple[3] + couple[4] + couple[5]
    return (couple, coupling)


def combine_neighbours(values, padded, couple, coupling, tau_step):
    beside = couple[0] * padded[:, 2:, 1:-1, 1:-1] + couple[1] * padded[:, :-2, 1:-1, 1:-1]
    beside = beside + couple[2] * padded[:, 1:-1, 2:, 1:-1] + couple[3] * padded[:, 1:-1, :-2, 1:-1]
    beside = beside + couple[4] * padded[:, 1:-1, 1:-1, 2:] + couple[5] * padded[:, 1:-1, 1:-1, :-2]
    return (1.0 + tau_step * coupling) * values - tau_step * beside


def apply_operator(values, couple, coupling, tau_step):
    bordered = padded_2(values, (("sx", 1), ("sy", 2)), 1)
    padded = jnp.pad(bordered, ((0, 0), (0, 0), (0, 0), (1, 1)))
    return combine_neighbours(values, padded, couple, coupling, tau_step)


def previous_end(values):
    return shifted(values[-1], "tm", 1)


def smooth(values, source, couple, coupling, tau_step, from_zero):
    diagonal = 1.0 + tau_step * coupling
    factor = relax_weight / diagonal
    if from_zero:
        applied = jnp.zeros_like(values)
        running = jnp.zeros_like(values[0])
    else:
        applied = apply_operator(values, couple, coupling, tau_step)
        running = previous_end(values)
    update = values + relax_weight * (source - applied) / diagonal
    results = []
    for position in range(values.shape[0]):
        running = update[position] + factor * running
        results.append(running)
    return jnp.stack(results, axis=0)


def defect(values, source, couple, coupling, tau_step):
    applied = apply_operator(values, couple, coupling, tau_step)
    earlier = jnp.concatenate([previous_end(values)[None], values[:-1]], axis=0)
    return source + earlier - applied


def chain_solve(update, factor):

    def relay_turn(turn_index, relayed):
        before = shifted(relayed, "tm", 2)
        return update + factor * before

    return lax.fori_loop(0, lax.axis_size("tm") // 2, relay_turn, jnp.zeros_like(update))


def coarse_sweep(values, source, couple, coupling, tau_step, from_zero):
    diagonal = 1.0 + tau_step * coupling
    factor = relax_weight / diagonal
    if from_zero:
        applied = jnp.zeros_like(values)
    else:
        applied = apply_operator(values, couple, coupling, tau_step)
    update = values + relax_weight * (source - applied) / diagonal
    return chain_solve(update[0], factor)[None]


def per_device(heat_source, conductivity, initial_iterate):
    couple, coupling = face_terms(conductivity)
    first = smooth(initial_iterate, heat_source, couple, coupling, fine_step, False)
    defect_fine = defect(first, heat_source, couple, coupling, fine_step)
    source_one = defect_fine[0::2] + defect_fine[1::2]
    error_one = smooth(
        jnp.zeros_like(source_one), source_one, couple, coupling, 2.0 * fine_step, True
    )
    defect_one = defect(error_one, source_one, couple, coupling, 2.0 * fine_step)
    source_two = defect_one[0::2] + defect_one[1::2]
    error_two = smooth(
        jnp.zeros_like(source_two), source_two, couple, coupling, 4.0 * fine_step, True
    )
    defect_two = defect(error_two, source_two, couple, coupling, 4.0 * fine_step)
    partner = partner_2(defect_two, "tm", 0)
    lower_first = lax.axis_index("tm") % 2 == 0
    source_three = jnp.where(lower_first, defect_two + partner, partner + defect_two)
    error_three = coarse_sweep(
        jnp.zeros_like(source_three), source_three, couple, coupling, 8.0 * fine_step, True
    )
    raised = coarse_sweep(error_three, source_three, couple, coupling, 8.0 * fine_step, False)
    error_two = smooth(error_two + raised, source_two, couple, coupling, 4.0 * fine_step, False)
    error_one = smooth(
        error_one + jnp.repeat(error_two, 2, axis=0),
        source_one,
        couple,
        coupling,
        2.0 * fine_step,
        False,
    )
    solution = smooth(
        first + jnp.repeat(error_one, 2, axis=0), heat_source, couple, coupling, fine_step, False
    )
    return (solution, defect(solution, heat_source, couple, coupling, fine_step))


def solution(mesh):
    placed = (P("tm", "sx", "sy", None), P("sx", "sy", None), P("tm", "sx", "sy", None))
    return jax.shard_map(
        per_device,
        mesh=mesh,
        in_specs=placed,
        out_specs=(P("tm", "sx", "sy", None), P("tm", "sx", "sy", None)),
        check_vma=False,
    )
```

profile of v0, /device:TPU:27, one launch (start us, length us, event | category | flops | bytes accessed | tf_op | source)
XLA Modules:
  0.0 188.2 jit_solution(14968199204807554019)
XLA Ops:
  1.4 1.3 collective-permute-start.1
  2.7 4.0 %collective-permute-start = (f32[1,16,128]{2,1,0:T(8,128)S(1)}, f32[1,16,128]{2,1,0:T(8,128)S(1)}, u32[]{:S(2)}, u32[]{:S(2)}) collective-permute-start(f32[1,16,128]{2,1,0:T(8,128)S(1)} %get-tuple-element.88), channel_id=1, source_target_pairs={{4,0},{8,4},{12,8},{5,1},{9,5},{13,9},{6,2},{10,6},{14,10},{7,3},{... | collective-permute-start | bytes 24584 | tf_op jit(solution)/shard_map/ppermute | solution.py:20
  7.5 1.3 collective-permute-start.5
  8.8 4.0 %collective-permute-start.4 = (f32[4,1,16,128]{3,2,1,0:T(8,128)S(1)}, f32[4,1,16,128]{3,2,1,0:T(8,128)S(1)}, u32[]{:S(2)}, u32[]{:S(2)}) collective-permute-start(f32[4,1,16,128]{3,2,1,0:T(8,128)S(1)} %get-tuple-element.60), channel_id=1, source_target_pairs={{4,0},{8,4},{12,8},{5,1},{9,5},{13,9},{6,2},{10,6},{14,10},{7,3},{... | collective-permute-start | bytes 98312 | tf_op jit(solution)/shard_map/ppermute | solution.py:20
  13.8 3.7 %collective-permute-start.2 = (f32[18,1,128]{2,1,0:T(1,128)S(1)}, f32[18,1,128]{2,1,0:T(1,128)S(1)}, u32[]{:S(2)}, u32[]{:S(2)}) collective-permute-start(f32[18,1,128]{2,1,0:T(1,128)S(1)} %get-tuple-element.79), channel_id=1, source_target_pairs={{1,0},{2,1},{3,2},{5,4},{6,5},{7,6},{9,8},{10,9},{11,10},{13,12},{... | collective-permute-start | bytes 27656 | tf_op jit(solution)/shard_map/ppermute | solution.py:20
  17.5 3.0 %collective-permute-start.3 = (f32[18,1,128]{2,1,0:T(1,128)S(1)}, f32[18,1,128]{2,1,0:T(1,128)S(1)}, u32[]{:S(2)}, u32[]{:S(2)}) collective-permute-start(f32[18,1,128]{2,1,0:T(1,128)S(1)} %get-tuple-element.78), channel_id=1, source_target_pairs={{0,1},{1,2},{2,3},{4,5},{5,6},{6,7},{8,9},{9,10},{10,11},{12,13},{... | collective-permute-start | bytes 27656 | tf_op jit(solution)/shard_map/ppermute | solution.py:18
  21.5 1.3 collective-permute-start.8
  23.2 1.9 %collective-permute-start.6 = (f32[4,18,1,128]{3,2,1,0:T(1,128)S(1)}, f32[4,18,1,128]{3,2,1,0:T(1,128)S(1)}, u32[]{:S(2)}, u32[]{:S(2)}) collective-permute-start(f32[4,18,1,128]{3,2,1,0:T(1,128)S(1)} %get-tuple-element.51), channel_id=1, source_target_pairs={{1,0},{2,1},{3,2},{5,4},{6,5},{7,6},{9,8},{10,9},{11,10},{13,12},{... | collective-permute-start | bytes 110600 | tf_op jit(solution)/shard_map/ppermute | solution.py:20
  25.2 3.8 %collective-permute-start.7 = (f32[4,18,1,128]{3,2,1,0:T(1,128)S(1)}, f32[4,18,1,128]{3,2,1,0:T(1,128)S(1)}, u32[]{:S(2)}, u32[]{:S(2)}) collective-permute-start(f32[4,18,1,128]{3,2,1,0:T(1,128)S(1)} %get-tuple-element.50), channel_id=1, source_target_pairs={{0,1},{1,2},{2,3},{4,5},{5,6},{6,7},{8,9},{9,10},{10,11},{12,13},{... | collective-permute-start | bytes 110600 | tf_op jit(solution)/shard_map/ppermute | solution.py:18
  31.6 2.1 %collective-permute-start.10 = (f32[4,1,16,128]{3,2,1,0:T(8,128)S(1)}, f32[4,1,16,128]{3,2,1,0:T(8,128)S(1)}, u32[]{:S(2)}, u32[]{:S(2)}) collective-permute-start(f32[4,1,16,128]{3,2,1,0:T(8,128)S(1)} %get-tuple-element.59), channel_id=1, source_target_pairs={{4,0},{8,4},{12,8},{5,1},{9,5},{13,9},{6,2},{10,6},{14,10},{7,3},{... | collective-permute-start | bytes 98312 | tf_op jit(solution)/shard_map/ppermute | solution.py:20
  33.7 1.3 collective-permute-start.11
  35.0 3.3 %collective-permute-done.11 = f32[4,1,16,128]{3,2,1,0:T(8,128)S(1)} collective-permute-done((f32[4,1,16,128]{3,2,1,0:T(8,128)S(1)}, f32[4,1,16,128]{3,2,1,0:T(8,128)S(1)}, u32[]{:S(2)}, u32[]{:S(2)}) %collective-permute-start.11) | collective-permute-done | bytes 32800 | tf_op jit(solution)/shard_map/ppermute | solution.py:18
  38.4 1.9 %collective-permute-start.12 = (f32[4,18,1,128]{3,2,1,0:T(1,128)S(1)}, f32[4,18,1,128]{3,2,1,0:T(1,128)S(1)}, u32[]{:S(2)}, u32[]{:S(2)}) collective-permute-start(f32[4,18,1,128]{3,2,1,0:T(1,128)S(1)} %get-tuple-element.49), channel_id=1, source_target_pairs={{1,0},{2,1},{3,2},{5,4},{6,5},{7,6},{9,8},{10,9},{11,10},{13,12},{... | collective-permute-start | bytes 110600 | tf_op jit(solution)/shard_map/ppermute | solution.py:20
  40.3 5.7 %collective-permute-start.13 = (f32[4,18,1,128]{3,2,1,0:T(1,128)S(1)}, f32[4,18,1,128]{3,2,1,0:T(1,128)S(1)}, u32[]{:S(2)}, u32[]{:S(2)}) collective-permute-start(f32[4,18,1,128]{3,2,1,0:T(1,128)S(1)} %get-tuple-element.48), channel_id=1, source_target_pairs={{0,1},{1,2},{2,3},{4,5},{5,6},{6,7},{8,9},{9,10},{10,11},{12,13},{... | collective-permute-start | bytes 110600 | tf_op jit(solution)/shard_map/ppermute | solution.py:18
  46.0 1.3 collective-permute-start.9
  47.5 4.3 %collective-permute-done.9 = f32[16,16,128]{2,1,0:T(8,128)S(1)} collective-permute-done((f32[16,16,128]{2,1,0:T(8,128)S(1)}, f32[16,16,128]{2,1,0:T(8,128)S(1)}, u32[]{:S(2)}, u32[]{:S(2)}) %collective-permute-start.9) | collective-permute-done | bytes 131104 | tf_op jit(solution)/shard_map/ppermute | solution.py:30
  52.3 2.1 %collective-permute-start.15 = (f32[2,1,16,128]{3,2,1,0:T(8,128)S(1)}, f32[2,1,16,128]{3,2,1,0:T(8,128)S(1)}, u32[]{:S(2)}, u32[]{:S(2)}) collective-permute-start(f32[2,1,16,128]{3,2,1,0:T(8,128)S(1)} %get-tuple-element.71), channel_id=1, source_target_pairs={{4,0},{8,4},{12,8},{5,1},{9,5},{13,9},{6,2},{10,6},{14,10},{7,3},{... | collective-permute-start | bytes 49160 | tf_op jit(solution)/shard_map/ppermute | solution.py:20
  54.4 1.3 collective-permute-start.16
  55.7 3.2 %collective-permute-done.16 = f32[2,1,16,128]{3,2,1,0:T(8,128)S(1)} collective-permute-done((f32[2,1,16,128]{3,2,1,0:T(8,128)S(1)}, f32[2,1,16,128]{3,2,1,0:T(8,128)S(1)}, u32[]{:S(2)}, u32[]{:S(2)}) %collective-permute-start.16) | collective-permute-done | bytes 16416 | tf_op jit(solution)/shard_map/ppermute | solution.py:18
  58.9 1.9 %collective-permute-start.17 = (f32[2,18,1,128]{3,2,1,0:T(1,128)S(1)}, f32[2,18,1,128]{3,2,1,0:T(1,128)S(1)}, u32[]{:S(2)}, u32[]{:S(2)}) collective-permute-start(f32[2,18,1,128]{3,2,1,0:T(1,128)S(1)} %get-tuple-element.67), channel_id=1, source_target_pairs={{1,0},{2,1},{3,2},{5,4},{6,5},{7,6},{9,8},{10,9},{11,10},{13,12},{... | collective-permute-start | bytes 55304 | tf_op jit(solution)/shard_map/ppermute | solution.py:20
  60.8 5.0 %collective-permute-start.18 = (f32[2,18,1,128]{3,2,1,0:T(1,128)S(1)}, f32[2,18,1,128]{3,2,1,0:T(1,128)S(1)}, u32[]{:S(2)}, u32[]{:S(2)}) collective-permute-start(f32[2,18,1,128]{3,2,1,0:T(1,128)S(1)} %get-tuple-element.66), channel_id=1, source_target_pairs={{0,1},{1,2},{2,3},{4,5},{5,6},{6,7},{8,9},{9,10},{10,11},{12,13},{... | collective-permute-start | bytes 55304 | tf_op jit(solution)/shard_map/ppermute | solution.py:18
  65.8 1.3 collective-permute-start.14
  67.6 3.9 %collective-permute-done.14 = f32[16,16,128]{2,1,0:T(8,128)S(1)} collective-permute-done((f32[16,16,128]{2,1,0:T(8,128)S(1)}, f32[16,16,128]{2,1,0:T(8,128)S(1)}, u32[]{:S(2)}, u32[]{:S(2)}) %collective-permute-start.14) | collective-permute-done | bytes 131104 | tf_op jit(solution)/shard_map/ppermute | solution.py:30
  72.0 1.6 collective-permute-start.20
  73.6 1.3 collective-permute-start.21
  74.9 3.1 %collective-permute-done.21 = f32[1,1,16,128]{3,2,1,0:T(8,128)S(1)} collective-permute-done((f32[1,1,16,128]{3,2,1,0:T(8,128)S(1)}, f32[1,1,16,128]{3,2,1,0:T(8,128)S(1)}, u32[]{:S(2)}, u32[]{:S(2)}) %collective-permute-start.21) | collective-permute-done | bytes 8224 | tf_op jit(solution)/shard_map/ppermute | solution.py:18
  78.0 2.2 %collective-permute-start.22 = (f32[1,18,1,128]{3,2,1,0:T(1,128)S(1)}, f32[1,18,1,128]{3,2,1,0:T(1,128)S(1)}, u32[]{:S(2)}, u32[]{:S(2)}) collective-permute-start(f32[1,18,1,128]{3,2,1,0:T(1,128)S(1)} %get-tuple-element.77), channel_id=1, source_target_pairs={{1,0},{2,1},{3,2},{5,4},{6,5},{7,6},{9,8},{10,9},{11,10},{13,12},{... | collective-permute-start | bytes 27656 | tf_op jit(solution)/shard_map/ppermute | solution.py:20
  80.3 4.7 %collective-permute-start.23 = (f32[1,18,1,128]{3,2,1,0:T(1,128)S(1)}, f32[1,18,1,128]{3,2,1,0:T(1,128)S(1)}, u32[]{:S(2)}, u32[]{:S(2)}) collective-permute-start(f32[1,18,1,128]{3,2,1,0:T(1,128)S(1)} %get-tuple-element.76), channel_id=1, source_target_pairs={{0,1},{1,2},{2,3},{4,5},{5,6},{6,7},{8,9},{9,10},{10,11},{12,13},{... | collective-permute-start | bytes 27656 | tf_op jit(solution)/shard_map/ppermute | solution.py:18
  85.0 1.3 collective-permute-start.19
  87.2 3.4 %collective-permute-done.19 = f32[16,16,128]{2,1,0:T(8,128)S(1)} collective-permute-done((f32[16,16,128]{2,1,0:T(8,128)S(1)}, f32[16,16,128]{2,1,0:T(8,128)S(1)}, u32[]{:S(2)}, u32[]{:S(2)}) %collective-permute-start.19) | collective-permute-done | bytes 131104 | tf_op jit(solution)/shard_map/ppermute | solution.py:30
  90.9 4.5 %collective-permute-done.24 = f32[1,16,16,128]{3,2,1,0:T(8,128)S(1)} collective-permute-done((f32[1,16,16,128]{3,2,1,0:T(8,128)S(1)}, f32[1,16,16,128]{3,2,1,0:T(8,128)S(1)}, u32[]{:S(2)}, u32[]{:S(2)}) %collective-permute-start.24) | collective-permute-done | bytes 131104 | tf_op jit(solution)/shard_map/ppermute | solution.py:34
  95.5 1.7 collective-permute-start.26
  97.2 1.3 collective-permute-start.27
  98.5 3.1 %collective-permute-done.27 = f32[1,1,16,128]{3,2,1,0:T(8,128)S(1)} collective-permute-done((f32[1,1,16,128]{3,2,1,0:T(8,128)S(1)}, f32[1,1,16,128]{3,2,1,0:T(8,128)S(1)}, u32[]{:S(2)}, u32[]{:S(2)}) %collective-permute-start.27) | collective-permute-done | bytes 8224 | tf_op jit(solution)/shard_map/ppermute | solution.py:18
  101.6 3.4 %collective-permute-start.28 = (f32[1,18,1,128]{3,2,1,0:T(1,128)S(1)}, f32[1,18,1,128]{3,2,1,0:T(1,128)S(1)}, u32[]{:S(2)}, u32[]{:S(2)}) collective-permute-start(f32[1,18,1,128]{3,2,1,0:T(1,128)S(1)} %get-tuple-element.75), channel_id=1, source_target_pairs={{1,0},{2,1},{3,2},{5,4},{6,5},{7,6},{9,8},{10,9},{11,10},{13,12},{... | collective-permute-start | bytes 27656 | tf_op jit(solution)/shard_map/ppermute | solution.py:20
  105.0 3.9 %collective-permute-start.29 = (f32[1,18,1,128]{3,2,1,0:T(1,128)S(1)}, f32[1,18,1,128]{3,2,1,0:T(1,128)S(1)}, u32[]{:S(2)}, u32[]{:S(2)}) collective-permute-start(f32[1,18,1,128]{3,2,1,0:T(1,128)S(1)} %get-tuple-element.74), channel_id=1, source_target_pairs={{0,1},{1,2},{2,3},{4,5},{5,6},{6,7},{8,9},{9,10},{10,11},{12,13},{... | collective-permute-start | bytes 27656 | tf_op jit(solution)/shard_map/ppermute | solution.py:18
  110.2 1.6 collective-permute-start.30
  111.9 1.3 collective-permute-start.31
  113.2 3.1 %collective-permute-done.31 = f32[1,1,16,128]{3,2,1,0:T(8,128)S(1)} collective-permute-done((f32[1,1,16,128]{3,2,1,0:T(8,128)S(1)}, f32[1,1,16,128]{3,2,1,0:T(8,128)S(1)}, u32[]{:S(2)}, u32[]{:S(2)}) %collective-permute-start.31) | collective-permute-done | bytes 8224 | tf_op jit(solution)/shard_map/ppermute | solution.py:18
  116.3 1.9 %collective-permute-start.32 = (f32[1,18,1,128]{3,2,1,0:T(1,128)S(1)}, f32[1,18,1,128]{3,2,1,0:T(1,128)S(1)}, u32[]{:S(2)}, u32[]{:S(2)}) collective-permute-start(f32[1,18,1,128]{3,2,1,0:T(1,128)S(1)} %get-tuple-element.73), channel_id=1, source_target_pairs={{1,0},{2,1},{3,2},{5,4},{6,5},{7,6},{9,8},{10,9},{11,10},{13,12},{... | collective-permute-start | bytes 27656 | tf_op jit(solution)/shard_map/ppermute | solution.py:20
  118.2 5.6 %collective-permute-start.33 = (f32[1,18,1,128]{3,2,1,0:T(1,128)S(1)}, f32[1,18,1,128]{3,2,1,0:T(1,128)S(1)}, u32[]{:S(2)}, u32[]{:S(2)}) collective-permute-start(f32[1,18,1,128]{3,2,1,0:T(1,128)S(1)} %get-tuple-element.72), channel_id=1, source_target_pairs={{0,1},{1,2},{2,3},{4,5},{5,6},{6,7},{8,9},{9,10},{10,11},{12,13},{... | collective-permute-start | bytes 27656 | tf_op jit(solution)/shard_map/ppermute | solution.py:18
  123.8 1.3 collective-permute-start.34
  125.4 4.1 %collective-permute-done.34 = f32[16,16,128]{2,1,0:T(8,128)S(1)} collective-permute-done((f32[16,16,128]{2,1,0:T(8,128)S(1)}, f32[16,16,128]{2,1,0:T(8,128)S(1)}, u32[]{:S(2)}, u32[]{:S(2)}) %collective-permute-start.34) | collective-permute-done | bytes 131104 | tf_op jit(solution)/shard_map/ppermute | solution.py:30
  129.8 1.6 collective-permute-start.35
  131.5 1.3 collective-permute-start.36
  132.8 3.2 %collective-permute-done.36 = f32[2,1,16,128]{3,2,1,0:T(8,128)S(1)} collective-permute-done((f32[2,1,16,128]{3,2,1,0:T(8,128)S(1)}, f32[2,1,16,128]{3,2,1,0:T(8,128)S(1)}, u32[]{:S(2)}, u32[]{:S(2)}) %collective-permute-start.36) | collective-permute-done | bytes 16416 | tf_op jit(solution)/shard_map/ppermute | solution.py:18
  136.0 1.9 %collective-permute-start.37 = (f32[2,18,1,128]{3,2,1,0:T(1,128)S(1)}, f32[2,18,1,128]{3,2,1,0:T(1,128)S(1)}, u32[]{:S(2)}, u32[]{:S(2)}) collective-permute-start(f32[2,18,1,128]{3,2,1,0:T(1,128)S(1)} %get-tuple-element.65), channel_id=1, source_target_pairs={{1,0},{2,1},{3,2},{5,4},{6,5},{7,6},{9,8},{10,9},{11,10},{13,12},{... | collective-permute-start | bytes 55304 | tf_op jit(solution)/shard_map/ppermute | solution.py:20
  137.9 5.0 %collective-permute-start.38 = (f32[2,18,1,128]{3,2,1,0:T(1,128)S(1)}, f32[2,18,1,128]{3,2,1,0:T(1,128)S(1)}, u32[]{:S(2)}, u32[]{:S(2)}) collective-permute-start(f32[2,18,1,128]{3,2,1,0:T(1,128)S(1)} %get-tuple-element.64), channel_id=1, source_target_pairs={{0,1},{1,2},{2,3},{4,5},{5,6},{6,7},{8,9},{9,10},{10,11},{12,13},{... | collective-permute-start | bytes 55304 | tf_op jit(solution)/shard_map/ppermute | solution.py:18
  142.9 1.3 collective-permute-start.39
  145.0 3.6 %collective-permute-done.39 = f32[16,16,128]{2,1,0:T(8,128)S(1)} collective-permute-done((f32[16,16,128]{2,1,0:T(8,128)S(1)}, f32[16,16,128]{2,1,0:T(8,128)S(1)}, u32[]{:S(2)}, u32[]{:S(2)}) %collective-permute-start.39) | collective-permute-done | bytes 131104 | tf_op jit(solution)/shard_map/ppermute | solution.py:30
  148.8 1.6 collective-permute-start.40
  150.4 1.3 collective-permute-start.41
  151.7 3.3 %collective-permute-done.41 = f32[4,1,16,128]{3,2,1,0:T(8,128)S(1)} collective-permute-done((f32[4,1,16,128]{3,2,1,0:T(8,128)S(1)}, f32[4,1,16,128]{3,2,1,0:T(8,128)S(1)}, u32[]{:S(2)}, u32[]{:S(2)}) %collective-permute-start.41) | collective-permute-done | bytes 32800 | tf_op jit(solution)/shard_map/ppermute | solution.py:18
  155.1 2.2 %collective-permute-start.42 = (f32[4,18,1,128]{3,2,1,0:T(1,128)S(1)}, f32[4,18,1,128]{3,2,1,0:T(1,128)S(1)}, u32[]{:S(2)}, u32[]{:S(2)}) collective-permute-start(f32[4,18,1,128]{3,2,1,0:T(1,128)S(1)} %get-tuple-element.47), channel_id=1, source_target_pairs={{1,0},{2,1},{3,2},{5,4},{6,5},{7,6},{9,8},{10,9},{11,10},{13,12},{... | collective-permute-start | bytes 110600 | tf_op jit(solution)/shard_map/ppermute | solution.py:20
  157.3 4.7 %collective-permute-start.43 = (f32[4,18,1,128]{3,2,1,0:T(1,128)S(1)}, f32[4,18,1,128]{3,2,1,0:T(1,128)S(1)}, u32[]{:S(2)}, u32[]{:S(2)}) collective-permute-start(f32[4,18,1,128]{3,2,1,0:T(1,128)S(1)} %get-tuple-element.46), channel_id=1, source_target_pairs={{0,1},{1,2},{2,3},{4,5},{5,6},{6,7},{8,9},{9,10},{10,11},{12,13},{... | collective-permute-start | bytes 110600 | tf_op jit(solution)/shard_map/ppermute | solution.py:18
  162.1 1.3 collective-permute-start.44
  164.8 3.0 %collective-permute-done.44 = f32[16,16,128]{2,1,0:T(8,128)S(1)} collective-permute-done((f32[16,16,128]{2,1,0:T(8,128)S(1)}, f32[16,16,128]{2,1,0:T(8,128)S(1)}, u32[]{:S(2)}, u32[]{:S(2)}) %collective-permute-start.44) | collective-permute-done | bytes 131104 | tf_op jit(solution)/shard_map/ppermute | solution.py:30
  168.0 1.6 collective-permute-start.46
  169.6 1.3 collective-permute-start.47
  170.9 3.3 %collective-permute-done.47 = f32[4,1,16,128]{3,2,1,0:T(8,128)S(1)} collective-permute-done((f32[4,1,16,128]{3,2,1,0:T(8,128)S(1)}, f32[4,1,16,128]{3,2,1,0:T(8,128)S(1)}, u32[]{:S(2)}, u32[]{:S(2)}) %collective-permute-start.47) | collective-permute-done | bytes 32800 | tf_op jit(solution)/shard_map/ppermute | solution.py:18
  174.3 2.2 %collective-permute-start.48 = (f32[4,18,1,128]{3,2,1,0:T(1,128)S(1)}, f32[4,18,1,128]{3,2,1,0:T(1,128)S(1)}, u32[]{:S(2)}, u32[]{:S(2)}) collective-permute-start(f32[4,18,1,128]{3,2,1,0:T(1,128)S(1)} %get-tuple-element.45), channel_id=1, source_target_pairs={{1,0},{2,1},{3,2},{5,4},{6,5},{7,6},{9,8},{10,9},{11,10},{13,12},{... | collective-permute-start | bytes 110600 | tf_op jit(solution)/shard_map/ppermute | solution.py:20
  176.6 4.7 %collective-permute-start.49 = (f32[4,18,1,128]{3,2,1,0:T(1,128)S(1)}, f32[4,18,1,128]{3,2,1,0:T(1,128)S(1)}, u32[]{:S(2)}, u32[]{:S(2)}) collective-permute-start(f32[4,18,1,128]{3,2,1,0:T(1,128)S(1)} %get-tuple-element.44), channel_id=1, source_target_pairs={{0,1},{1,2},{2,3},{4,5},{5,6},{6,7},{8,9},{9,10},{10,11},{12,13},{... | collective-permute-start | bytes 110600 | tf_op jit(solution)/shard_map/ppermute | solution.py:18
  181.3 1.3 collective-permute-start.45
  182.7 4.3 %collective-permute-done.45 = f32[16,16,128]{2,1,0:T(8,128)S(1)} collective-permute-done((f32[16,16,128]{2,1,0:T(8,128)S(1)}, f32[16,16,128]{2,1,0:T(8,128)S(1)}, u32[]{:S(2)}, u32[]{:S(2)}) %collective-permute-start.45) | collective-permute-done | bytes 131104 | tf_op jit(solution)/shard_map/ppermute | solution.py:30
  (109 shorter events, 15.2 us)
Async XLA Ops:
  0.6 28.3 %copy-start.3 = (f32[16,16,128]{2,1,0:T(8,128)S(1)}, f32[16,16,128]{2,1,0:T(8,128)}, u32[]{:S(2)}) copy-start(f32[16,16,128]{2,1,0:T(8,128)} %param.4) | copy-start | bytes 393220
  0.6 22.4 %copy-start.1 = (f32[4,16,16,128]{3,2,1,0:T(8,128)S(1)}, f32[4,16,16,128]{3,2,1,0:T(8,128)}, u32[]{:S(2)}) copy-start(f32[4,16,16,128]{3,2,1,0:T(8,128)} %param.5) | copy-start | bytes 1572868
  1.4 11.4 %collective-permute-start.1 = (f32[1,16,128]{2,1,0:T(8,128)S(1)}, f32[1,16,128]{2,1,0:T(8,128)S(1)}, u32[]{:S(2)}, u32[]{:S(2)}) collective-permute-start(f32[1,16,128]{2,1,0:T(8,128)S(1)} %get-tuple-element.89), channel_id=1, source_target_pairs={{0,4},{4,8},{8,12},{1,5},{5,9},{9,13},{2,6},{6,10},{10,14},{3,7},{... | collective-permute-start | bytes 24584 | tf_op jit(solution)/shard_map/ppermute | solution.py:18
  2.7 11.0 %collective-permute-start = (f32[1,16,128]{2,1,0:T(8,128)S(1)}, f32[1,16,128]{2,1,0:T(8,128)S(1)}, u32[]{:S(2)}, u32[]{:S(2)}) collective-permute-start(f32[1,16,128]{2,1,0:T(8,128)S(1)} %get-tuple-element.88), channel_id=1, source_target_pairs={{4,0},{8,4},{12,8},{5,1},{9,5},{13,9},{6,2},{10,6},{14,10},{7,3},{... | collective-permute-start | bytes 24584 | tf_op jit(solution)/shard_map/ppermute | solution.py:20
  7.5 15.5 %collective-permute-start.5 = (f32[4,1,16,128]{3,2,1,0:T(8,128)S(1)}, f32[4,1,16,128]{3,2,1,0:T(8,128)S(1)}, u32[]{:S(2)}, u32[]{:S(2)}) collective-permute-start(f32[4,1,16,128]{3,2,1,0:T(8,128)S(1)} %get-tuple-element.61), channel_id=1, source_target_pairs={{0,4},{4,8},{8,12},{1,5},{5,9},{9,13},{2,6},{6,10},{10,14},{3,7},{... | collective-permute-start | bytes 98312 | tf_op jit(solution)/shard_map/ppermute | solution.py:18
  8.8 14.3 %collective-permute-start.4 = (f32[4,1,16,128]{3,2,1,0:T(8,128)S(1)}, f32[4,1,16,128]{3,2,1,0:T(8,128)S(1)}, u32[]{:S(2)}, u32[]{:S(2)}) collective-permute-start(f32[4,1,16,128]{3,2,1,0:T(8,128)S(1)} %get-tuple-element.60), channel_id=1, source_target_pairs={{4,0},{8,4},{12,8},{5,1},{9,5},{13,9},{6,2},{10,6},{14,10},{7,3},{... | collective-permute-start | bytes 98312 | tf_op jit(solution)/shard_map/ppermute | solution.py:20
  13.8 9.0 %collective-permute-start.2 = (f32[18,1,128]{2,1,0:T(1,128)S(1)}, f32[18,1,128]{2,1,0:T(1,128)S(1)}, u32[]{:S(2)}, u32[]{:S(2)}) collective-permute-start(f32[18,1,128]{2,1,0:T(1,128)S(1)} %get-tuple-element.79), channel_id=1, source_target_pairs={{1,0},{2,1},{3,2},{5,4},{6,5},{7,6},{9,8},{10,9},{11,10},{13,12},{... | collective-permute-start | bytes 27656 | tf_op jit(solution)/shard_map/ppermute | solution.py:20
  17.5 5.3 %collective-permute-start.3 = (f32[18,1,128]{2,1,0:T(1,128)S(1)}, f32[18,1,128]{2,1,0:T(1,128)S(1)}, u32[]{:S(2)}, u32[]{:S(2)}) collective-permute-start(f32[18,1,128]{2,1,0:T(1,128)S(1)} %get-tuple-element.78), channel_id=1, source_target_pairs={{0,1},{1,2},{2,3},{4,5},{5,6},{6,7},{8,9},{9,10},{10,11},{12,13},{... | collective-permute-start | bytes 27656 | tf_op jit(solution)/shard_map/ppermute | solution.py:18
  21.5 9.9 %collective-permute-start.8 = (f32[16,16,128]{2,1,0:T(8,128)S(1)}, f32[16,16,128]{2,1,0:T(8,128)S(1)}, u32[]{:S(2)}, u32[]{:S(2)}) collective-permute-start(f32[16,16,128]{2,1,0:T(8,128)S(1)} %slice_bitcast_fusion.14), channel_id=1, source_target_pairs={{0,16},{1,17},{2,18},{3,19},{4,20},{5,21},{6,22},{7,23},{8,24},{9,... | collective-permute-start | bytes 393224 | tf_op jit(solution)/shard_map/ppermute | solution.py:30
  23.2 5.9 %collective-permute-start.6 = (f32[4,18,1,128]{3,2,1,0:T(1,128)S(1)}, f32[4,18,1,128]{3,2,1,0:T(1,128)S(1)}, u32[]{:S(2)}, u32[]{:S(2)}) collective-permute-start(f32[4,18,1,128]{3,2,1,0:T(1,128)S(1)} %get-tuple-element.51), channel_id=1, source_target_pairs={{1,0},{2,1},{3,2},{5,4},{6,5},{7,6},{9,8},{10,9},{11,10},{13,12},{... | collective-permute-start | bytes 110600 | tf_op jit(solution)/shard_map/ppermute | solution.py:20
  25.1 5.7 %copy-start = (f32[4,16,16,128]{3,2,1,0:T(8,128)S(1)}, f32[4,16,16,128]{3,2,1,0:T(8,128)}, u32[]{:S(2)}) copy-start(f32[4,16,16,128]{3,2,1,0:T(8,128)} %param.3) | copy-start | bytes 1572868
  25.2 4.8 %collective-permute-start.7 = (f32[4,18,1,128]{3,2,1,0:T(1,128)S(1)}, f32[4,18,1,128]{3,2,1,0:T(1,128)S(1)}, u32[]{:S(2)}, u32[]{:S(2)}) collective-permute-start(f32[4,18,1,128]{3,2,1,0:T(1,128)S(1)} %get-tuple-element.50), channel_id=1, source_target_pairs={{0,1},{1,2},{2,3},{4,5},{5,6},{6,7},{8,9},{9,10},{10,11},{12,13},{... | collective-permute-start | bytes 110600 | tf_op jit(solution)/shard_map/ppermute | solution.py:18
  31.6 3.4 %collective-permute-start.10 = (f32[4,1,16,128]{3,2,1,0:T(8,128)S(1)}, f32[4,1,16,128]{3,2,1,0:T(8,128)S(1)}, u32[]{:S(2)}, u32[]{:S(2)}) collective-permute-start(f32[4,1,16,128]{3,2,1,0:T(8,128)S(1)} %get-tuple-element.59), channel_id=1, source_target_pairs={{4,0},{8,4},{12,8},{5,1},{9,5},{13,9},{6,2},{10,6},{14,10},{7,3},{... | collective-permute-start | bytes 98312 | tf_op jit(solution)/shard_map/ppermute | solution.py:20
  33.7 4.7 %collective-permute-start.11 = (f32[4,1,16,128]{3,2,1,0:T(8,128)S(1)}, f32[4,1,16,128]{3,2,1,0:T(8,128)S(1)}, u32[]{:S(2)}, u32[]{:S(2)}) collective-permute-start(f32[4,1,16,128]{3,2,1,0:T(8,128)S(1)} %get-tuple-element.58), channel_id=1, source_target_pairs={{0,4},{4,8},{8,12},{1,5},{5,9},{9,13},{2,6},{6,10},{10,14},{3,7},{... | collective-permute-start | bytes 98312 | tf_op jit(solution)/shard_map/ppermute | solution.py:18
  38.4 8.9 %collective-permute-start.12 = (f32[4,18,1,128]{3,2,1,0:T(1,128)S(1)}, f32[4,18,1,128]{3,2,1,0:T(1,128)S(1)}, u32[]{:S(2)}, u32[]{:S(2)}) collective-permute-start(f32[4,18,1,128]{3,2,1,0:T(1,128)S(1)} %get-tuple-element.49), channel_id=1, source_target_pairs={{1,0},{2,1},{3,2},{5,4},{6,5},{7,6},{9,8},{10,9},{11,10},{13,12},{... | collective-permute-start | bytes 110600 | tf_op jit(solution)/shard_map/ppermute | solution.py:20
  40.3 7.0 %collective-permute-start.13 = (f32[4,18,1,128]{3,2,1,0:T(1,128)S(1)}, f32[4,18,1,128]{3,2,1,0:T(1,128)S(1)}, u32[]{:S(2)}, u32[]{:S(2)}) collective-permute-start(f32[4,18,1,128]{3,2,1,0:T(1,128)S(1)} %get-tuple-element.48), channel_id=1, source_target_pairs={{0,1},{1,2},{2,3},{4,5},{5,6},{6,7},{8,9},{9,10},{10,11},{12,13},{... | collective-permute-start | bytes 110600 | tf_op jit(solution)/shard_map/ppermute | solution.py:18
  46.0 5.7 %collective-permute-start.9 = (f32[16,16,128]{2,1,0:T(8,128)S(1)}, f32[16,16,128]{2,1,0:T(8,128)S(1)}, u32[]{:S(2)}, u32[]{:S(2)}) collective-permute-start(f32[16,16,128]{2,1,0:T(8,128)S(1)} %get-tuple-element.86), channel_id=1, source_target_pairs={{0,16},{1,17},{2,18},{3,19},{4,20},{5,21},{6,22},{7,23},{8,24},{9,... | collective-permute-start | bytes 393224 | tf_op jit(solution)/shard_map/ppermute | solution.py:30
  52.3 3.4 %collective-permute-start.15 = (f32[2,1,16,128]{3,2,1,0:T(8,128)S(1)}, f32[2,1,16,128]{3,2,1,0:T(8,128)S(1)}, u32[]{:S(2)}, u32[]{:S(2)}) collective-permute-start(f32[2,1,16,128]{3,2,1,0:T(8,128)S(1)} %get-tuple-element.71), channel_id=1, source_target_pairs={{4,0},{8,4},{12,8},{5,1},{9,5},{13,9},{6,2},{10,6},{14,10},{7,3},{... | collective-permute-start | bytes 49160 | tf_op jit(solution)/shard_map/ppermute | solution.py:20
  54.4 4.5 %collective-permute-start.16 = (f32[2,1,16,128]{3,2,1,0:T(8,128)S(1)}, f32[2,1,16,128]{3,2,1,0:T(8,128)S(1)}, u32[]{:S(2)}, u32[]{:S(2)}) collective-permute-start(f32[2,1,16,128]{3,2,1,0:T(8,128)S(1)} %get-tuple-element.70), channel_id=1, source_target_pairs={{0,4},{4,8},{8,12},{1,5},{5,9},{9,13},{2,6},{6,10},{10,14},{3,7},{... | collective-permute-start | bytes 49160 | tf_op jit(solution)/shard_map/ppermute | solution.py:18
  58.9 8.2 %collective-permute-start.17 = (f32[2,18,1,128]{3,2,1,0:T(1,128)S(1)}, f32[2,18,1,128]{3,2,1,0:T(1,128)S(1)}, u32[]{:S(2)}, u32[]{:S(2)}) collective-permute-start(f32[2,18,1,128]{3,2,1,0:T(1,128)S(1)} %get-tuple-element.67), channel_id=1, source_target_pairs={{1,0},{2,1},{3,2},{5,4},{6,5},{7,6},{9,8},{10,9},{11,10},{13,12},{... | collective-permute-start | bytes 55304 | tf_op jit(solution)/shard_map/ppermute | solution.py:20
  60.8 6.3 %collective-permute-start.18 = (f32[2,18,1,128]{3,2,1,0:T(1,128)S(1)}, f32[2,18,1,128]{3,2,1,0:T(1,128)S(1)}, u32[]{:S(2)}, u32[]{:S(2)}) collective-permute-start(f32[2,18,1,128]{3,2,1,0:T(1,128)S(1)} %get-tuple-element.66), channel_id=1, source_target_pairs={{0,1},{1,2},{2,3},{4,5},{5,6},{6,7},{8,9},{9,10},{10,11},{12,13},{... | collective-permute-start | bytes 55304 | tf_op jit(solution)/shard_map/ppermute | solution.py:18
  65.8 5.7 %collective-permute-start.14 = (f32[16,16,128]{2,1,0:T(8,128)S(1)}, f32[16,16,128]{2,1,0:T(8,128)S(1)}, u32[]{:S(2)}, u32[]{:S(2)}) collective-permute-start(f32[16,16,128]{2,1,0:T(8,128)S(1)} %get-tuple-element.63), channel_id=1, source_target_pairs={{0,16},{1,17},{2,18},{3,19},{4,20},{5,21},{6,22},{7,23},{8,24},{9,... | collective-permute-start | bytes 393224 | tf_op jit(solution)/shard_map/ppermute | solution.py:30
  72.0 3.0 %collective-permute-start.20 = (f32[1,1,16,128]{3,2,1,0:T(8,128)S(1)}, f32[1,1,16,128]{3,2,1,0:T(8,128)S(1)}, u32[]{:S(2)}, u32[]{:S(2)}) collective-permute-start(f32[1,1,16,128]{3,2,1,0:T(8,128)S(1)} %get-tuple-element.85), channel_id=1, source_target_pairs={{4,0},{8,4},{12,8},{5,1},{9,5},{13,9},{6,2},{10,6},{14,10},{7,3},{... | collective-permute-start | bytes 24584 | tf_op jit(solution)/shard_map/ppermute | solution.py:20
  73.6 4.4 %collective-permute-start.21 = (f32[1,1,16,128]{3,2,1,0:T(8,128)S(1)}, f32[1,1,16,128]{3,2,1,0:T(8,128)S(1)}, u32[]{:S(2)}, u32[]{:S(2)}) collective-permute-start(f32[1,1,16,128]{3,2,1,0:T(8,128)S(1)} %get-tuple-element.84), channel_id=1, source_target_pairs={{0,4},{4,8},{8,12},{1,5},{5,9},{9,13},{2,6},{6,10},{10,14},{3,7},{... | collective-permute-start | bytes 24584 | tf_op jit(solution)/shard_map/ppermute | solution.py:18
  78.0 8.9 %collective-permute-start.22 = (f32[1,18,1,128]{3,2,1,0:T(1,128)S(1)}, f32[1,18,1,128]{3,2,1,0:T(1,128)S(1)}, u32[]{:S(2)}, u32[]{:S(2)}) collective-permute-start(f32[1,18,1,128]{3,2,1,0:T(1,128)S(1)} %get-tuple-element.77), channel_id=1, source_target_pairs={{1,0},{2,1},{3,2},{5,4},{6,5},{7,6},{9,8},{10,9},{11,10},{13,12},{... | collective-permute-start | bytes 27656 | tf_op jit(solution)/shard_map/ppermute | solution.py:20
  80.3 6.7 %collective-permute-start.23 = (f32[1,18,1,128]{3,2,1,0:T(1,128)S(1)}, f32[1,18,1,128]{3,2,1,0:T(1,128)S(1)}, u32[]{:S(2)}, u32[]{:S(2)}) collective-permute-start(f32[1,18,1,128]{3,2,1,0:T(1,128)S(1)} %get-tuple-element.76), channel_id=1, source_target_pairs={{0,1},{1,2},{2,3},{4,5},{5,6},{6,7},{8,9},{9,10},{10,11},{12,13},{... | collective-permute-start | bytes 27656 | tf_op jit(solution)/shard_map/ppermute | solution.py:18
  85.0 5.7 %collective-permute-start.19 = (f32[16,16,128]{2,1,0:T(8,128)S(1)}, f32[16,16,128]{2,1,0:T(8,128)S(1)}, u32[]{:S(2)}, u32[]{:S(2)}) collective-permute-start(f32[16,16,128]{2,1,0:T(8,128)S(1)} %get-tuple-element.26), channel_id=1, source_target_pairs={{0,16},{1,17},{2,18},{3,19},{4,20},{5,21},{6,22},{7,23},{8,24},{9,... | collective-permute-start | bytes 393224 | tf_op jit(solution)/shard_map/ppermute | solution.py:30
  86.3 4.7 %collective-permute-start.25 = (f32[16,16,128]{2,1,0:T(8,128)S(1)}, f32[16,16,128]{2,1,0:T(8,128)S(1)}, u32[]{:S(2)}, u32[]{:S(2)}) collective-permute-start(f32[16,16,128]{2,1,0:T(8,128)S(1)} %broadcast.72), channel_id=1, source_target_pairs={} | collective-permute-start | bytes 393224 | tf_op jit(solution)/shard_map/while/body/eval_jaxpr/ppermute | solution.py:30
  90.9 4.6 %collective-permute-start.24 = (f32[1,16,16,128]{3,2,1,0:T(8,128)S(1)}, f32[1,16,16,128]{3,2,1,0:T(8,128)S(1)}, u32[]{:S(2)}, u32[]{:S(2)}) collective-permute-start(f32[1,16,16,128]{3,2,1,0:T(8,128)S(1)} %fusion.126), channel_id=1, source_target_pairs={{0,16},{16,0},{1,17},{17,1},{2,18},{18,2},{3,19},{19,3},{4,20},{20... | collective-permute-start | bytes 393224 | tf_op jit(solution)/shard_map/ppermute | solution.py:34
  95.5 3.0 %collective-permute-start.26 = (f32[1,1,16,128]{3,2,1,0:T(8,128)S(1)}, f32[1,1,16,128]{3,2,1,0:T(8,128)S(1)}, u32[]{:S(2)}, u32[]{:S(2)}) collective-permute-start(f32[1,1,16,128]{3,2,1,0:T(8,128)S(1)} %get-tuple-element.83), channel_id=1, source_target_pairs={{4,0},{8,4},{12,8},{5,1},{9,5},{13,9},{6,2},{10,6},{14,10},{7,3},{... | collective-permute-start | bytes 24584 | tf_op jit(solution)/shard_map/ppermute | solution.py:20
  97.2 4.4 %collective-permute-start.27 = (f32[1,1,16,128]{3,2,1,0:T(8,128)S(1)}, f32[1,1,16,128]{3,2,1,0:T(8,128)S(1)}, u32[]{:S(2)}, u32[]{:S(2)}) collective-permute-start(f32[1,1,16,128]{3,2,1,0:T(8,128)S(1)} %get-tuple-element.82), channel_id=1, source_target_pairs={{0,4},{4,8},{8,12},{1,5},{5,9},{9,13},{2,6},{6,10},{10,14},{3,7},{... | collective-permute-start | bytes 24584 | tf_op jit(solution)/shard_map/ppermute | solution.py:18
  101.6 7.3 %collective-permute-start.28 = (f32[1,18,1,128]{3,2,1,0:T(1,128)S(1)}, f32[1,18,1,128]{3,2,1,0:T(1,128)S(1)}, u32[]{:S(2)}, u32[]{:S(2)}) collective-permute-start(f32[1,18,1,128]{3,2,1,0:T(1,128)S(1)} %get-tuple-element.75), channel_id=1, source_target_pairs={{1,0},{2,1},{3,2},{5,4},{6,5},{7,6},{9,8},{10,9},{11,10},{13,12},{... | collective-permute-start | bytes 27656 | tf_op jit(solution)/shard_map/ppermute | solution.py:20
  105.0 4.7 %collective-permute-start.29 = (f32[1,18,1,128]{3,2,1,0:T(1,128)S(1)}, f32[1,18,1,128]{3,2,1,0:T(1,128)S(1)}, u32[]{:S(2)}, u32[]{:S(2)}) collective-permute-start(f32[1,18,1,128]{3,2,1,0:T(1,128)S(1)} %get-tuple-element.74), channel_id=1, source_target_pairs={{0,1},{1,2},{2,3},{4,5},{5,6},{6,7},{8,9},{9,10},{10,11},{12,13},{... | collective-permute-start | bytes 27656 | tf_op jit(solution)/shard_map/ppermute | solution.py:18
  110.2 3.0 %collective-permute-start.30 = (f32[1,1,16,128]{3,2,1,0:T(8,128)S(1)}, f32[1,1,16,128]{3,2,1,0:T(8,128)S(1)}, u32[]{:S(2)}, u32[]{:S(2)}) collective-permute-start(f32[1,1,16,128]{3,2,1,0:T(8,128)S(1)} %get-tuple-element.81), channel_id=1, source_target_pairs={{4,0},{8,4},{12,8},{5,1},{9,5},{13,9},{6,2},{10,6},{14,10},{7,3},{... | collective-permute-start | bytes 24584 | tf_op jit(solution)/shard_map/ppermute | solution.py:20
  111.9 4.4 %collective-permute-start.31 = (f32[1,1,16,128]{3,2,1,0:T(8,128)S(1)}, f32[1,1,16,128]{3,2,1,0:T(8,128)S(1)}, u32[]{:S(2)}, u32[]{:S(2)}) collective-permute-start(f32[1,1,16,128]{3,2,1,0:T(8,128)S(1)} %get-tuple-element.80), channel_id=1, source_target_pairs={{0,4},{4,8},{8,12},{1,5},{5,9},{9,13},{2,6},{6,10},{10,14},{3,7},{... | collective-permute-start | bytes 24584 | tf_op jit(solution)/shard_map/ppermute | solution.py:18
  116.3 8.9 %collective-permute-start.32 = (f32[1,18,1,128]{3,2,1,0:T(1,128)S(1)}, f32[1,18,1,128]{3,2,1,0:T(1,128)S(1)}, u32[]{:S(2)}, u32[]{:S(2)}) collective-permute-start(f32[1,18,1,128]{3,2,1,0:T(1,128)S(1)} %get-tuple-element.73), channel_id=1, source_target_pairs={{1,0},{2,1},{3,2},{5,4},{6,5},{7,6},{9,8},{10,9},{11,10},{13,12},{... | collective-permute-start | bytes 27656 | tf_op jit(solution)/shard_map/ppermute | solution.py:20
  118.2 6.9 %collective-permute-start.33 = (f32[1,18,1,128]{3,2,1,0:T(1,128)S(1)}, f32[1,18,1,128]{3,2,1,0:T(1,128)S(1)}, u32[]{:S(2)}, u32[]{:S(2)}) collective-permute-start(f32[1,18,1,128]{3,2,1,0:T(1,128)S(1)} %get-tuple-element.72), channel_id=1, source_target_pairs={{0,1},{1,2},{2,3},{4,5},{5,6},{6,7},{8,9},{9,10},{10,11},{12,13},{... | collective-permute-start | bytes 27656 | tf_op jit(solution)/shard_map/ppermute | solution.py:18
  123.8 5.7 %collective-permute-start.34 = (f32[16,16,128]{2,1,0:T(8,128)S(1)}, f32[16,16,128]{2,1,0:T(8,128)S(1)}, u32[]{:S(2)}, u32[]{:S(2)}) collective-permute-start(f32[16,16,128]{2,1,0:T(8,128)S(1)} %fusion.151), channel_id=1, source_target_pairs={{0,16},{1,17},{2,18},{3,19},{4,20},{5,21},{6,22},{7,23},{8,24},{9,... | collective-permute-start | bytes 393224 | tf_op jit(solution)/shard_map/ppermute | solution.py:30
  129.8 3.0 %collective-permute-start.35 = (f32[2,1,16,128]{3,2,1,0:T(8,128)S(1)}, f32[2,1,16,128]{3,2,1,0:T(8,128)S(1)}, u32[]{:S(2)}, u32[]{:S(2)}) collective-permute-start(f32[2,1,16,128]{3,2,1,0:T(8,128)S(1)} %get-tuple-element.69), channel_id=1, source_target_pairs={{4,0},{8,4},{12,8},{5,1},{9,5},{13,9},{6,2},{10,6},{14,10},{7,3},{... | collective-permute-start | bytes 49160 | tf_op jit(solution)/shard_map/ppermute | solution.py:20
  131.5 4.5 %collective-permute-start.36 = (f32[2,1,16,128]{3,2,1,0:T(8,128)S(1)}, f32[2,1,16,128]{3,2,1,0:T(8,128)S(1)}, u32[]{:S(2)}, u32[]{:S(2)}) collective-permute-start(f32[2,1,16,128]{3,2,1,0:T(8,128)S(1)} %get-tuple-element.68), channel_id=1, source_target_pairs={{0,4},{4,8},{8,12},{1,5},{5,9},{9,13},{2,6},{6,10},{10,14},{3,7},{... | collective-permute-start | bytes 49160 | tf_op jit(solution)/shard_map/ppermute | solution.py:18
  136.0 8.2 %collective-permute-start.37 = (f32[2,18,1,128]{3,2,1,0:T(1,128)S(1)}, f32[2,18,1,128]{3,2,1,0:T(1,128)S(1)}, u32[]{:S(2)}, u32[]{:S(2)}) collective-permute-start(f32[2,18,1,128]{3,2,1,0:T(1,128)S(1)} %get-tuple-element.65), channel_id=1, source_target_pairs={{1,0},{2,1},{3,2},{5,4},{6,5},{7,6},{9,8},{10,9},{11,10},{13,12},{... | collective-permute-start | bytes 55304 | tf_op jit(solution)/shard_map/ppermute | solution.py:20
  137.9 6.3 %collective-permute-start.38 = (f32[2,18,1,128]{3,2,1,0:T(1,128)S(1)}, f32[2,18,1,128]{3,2,1,0:T(1,128)S(1)}, u32[]{:S(2)}, u32[]{:S(2)}) collective-permute-start(f32[2,18,1,128]{3,2,1,0:T(1,128)S(1)} %get-tuple-element.64), channel_id=1, source_target_pairs={{0,1},{1,2},{2,3},{4,5},{5,6},{6,7},{8,9},{9,10},{10,11},{12,13},{... | collective-permute-start | bytes 55304 | tf_op jit(solution)/shard_map/ppermute | solution.py:18
  142.9 5.7 %collective-permute-start.39 = (f32[16,16,128]{2,1,0:T(8,128)S(1)}, f32[16,16,128]{2,1,0:T(8,128)S(1)}, u32[]{:S(2)}, u32[]{:S(2)}) collective-permute-start(f32[16,16,128]{2,1,0:T(8,128)S(1)} %slice_bitcast_fusion.6), channel_id=1, source_target_pairs={{0,16},{1,17},{2,18},{3,19},{4,20},{5,21},{6,22},{7,23},{8,24},{9,... | collective-permute-start | bytes 393224 | tf_op jit(solution)/shard_map/ppermute | solution.py:30
  148.8 3.0 %collective-permute-start.40 = (f32[4,1,16,128]{3,2,1,0:T(8,128)S(1)}, f32[4,1,16,128]{3,2,1,0:T(8,128)S(1)}, u32[]{:S(2)}, u32[]{:S(2)}) collective-permute-start(f32[4,1,16,128]{3,2,1,0:T(8,128)S(1)} %get-tuple-element.55), channel_id=1, source_target_pairs={{4,0},{8,4},{12,8},{5,1},{9,5},{13,9},{6,2},{10,6},{14,10},{7,3},{... | collective-permute-start | bytes 98312 | tf_op jit(solution)/shard_map/ppermute | solution.py:20
  150.4 4.7 %collective-permute-start.41 = (f32[4,1,16,128]{3,2,1,0:T(8,128)S(1)}, f32[4,1,16,128]{3,2,1,0:T(8,128)S(1)}, u32[]{:S(2)}, u32[]{:S(2)}) collective-permute-start(f32[4,1,16,128]{3,2,1,0:T(8,128)S(1)} %get-tuple-element.54), channel_id=1, source_target_pairs={{0,4},{4,8},{8,12},{1,5},{5,9},{9,13},{2,6},{6,10},{10,14},{3,7},{... | collective-permute-start | bytes 98312 | tf_op jit(solution)/shard_map/ppermute | solution.py:18
  155.1 8.2 %collective-permute-start.42 = (f32[4,18,1,128]{3,2,1,0:T(1,128)S(1)}, f32[4,18,1,128]{3,2,1,0:T(1,128)S(1)}, u32[]{:S(2)}, u32[]{:S(2)}) collective-permute-start(f32[4,18,1,128]{3,2,1,0:T(1,128)S(1)} %get-tuple-element.47), channel_id=1, source_target_pairs={{1,0},{2,1},{3,2},{5,4},{6,5},{7,6},{9,8},{10,9},{11,10},{13,12},{... | collective-permute-start | bytes 110600 | tf_op jit(solution)/shard_map/ppermute | solution.py:20
  157.3 6.0 %collective-permute-start.43 = (f32[4,18,1,128]{3,2,1,0:T(1,128)S(1)}, f32[4,18,1,128]{3,2,1,0:T(1,128)S(1)}, u32[]{:S(2)}, u32[]{:S(2)}) collective-permute-start(f32[4,18,1,128]{3,2,1,0:T(1,128)S(1)} %get-tuple-element.46), channel_id=1, source_target_pairs={{0,1},{1,2},{2,3},{4,5},{5,6},{6,7},{8,9},{9,10},{10,11},{12,13},{... | collective-permute-start | bytes 110600 | tf_op jit(solution)/shard_map/ppermute | solution.py:18
  162.1 5.7 %collective-permute-start.44 = (f32[16,16,128]{2,1,0:T(8,128)S(1)}, f32[16,16,128]{2,1,0:T(8,128)S(1)}, u32[]{:S(2)}, u32[]{:S(2)}) collective-permute-start(f32[16,16,128]{2,1,0:T(8,128)S(1)} %slice_bitcast_fusion.3), channel_id=1, source_target_pairs={{0,16},{1,17},{2,18},{3,19},{4,20},{5,21},{6,22},{7,23},{8,24},{9,... | collective-permute-start | bytes 393224 | tf_op jit(solution)/shard_map/ppermute | solution.py:30
  167.9 20.3 %copy-start.2 = (f32[4,16,16,128]{3,2,1,0:T(8,128)}, f32[4,16,16,128]{3,2,1,0:T(8,128)S(1)}, u32[]{:S(2)}) copy-start(f32[4,16,16,128]{3,2,1,0:T(8,128)S(1)} %pad_maximum_fusion.55) | copy-start | bytes 1572868
  168.0 3.0 %collective-permute-start.46 = (f32[4,1,16,128]{3,2,1,0:T(8,128)S(1)}, f32[4,1,16,128]{3,2,1,0:T(8,128)S(1)}, u32[]{:S(2)}, u32[]{:S(2)}) collective-permute-start(f32[4,1,16,128]{3,2,1,0:T(8,128)S(1)} %get-tuple-element.53), channel_id=1, source_target_pairs={{4,0},{8,4},{12,8},{5,1},{9,5},{13,9},{6,2},{10,6},{14,10},{7,3},{... | collective-permute-start | bytes 98312 | tf_op jit(solution)/shard_map/ppermute | solution.py:20
  169.6 4.7 %collective-permute-start.47 = (f32[4,1,16,128]{3,2,1,0:T(8,128)S(1)}, f32[4,1,16,128]{3,2,1,0:T(8,128)S(1)}, u32[]{:S(2)}, u32[]{:S(2)}) collective-permute-start(f32[4,1,16,128]{3,2,1,0:T(8,128)S(1)} %get-tuple-element.52), channel_id=1, source_target_pairs={{0,4},{4,8},{8,12},{1,5},{5,9},{9,13},{2,6},{6,10},{10,14},{3,7},{... | collective-permute-start | bytes 98312 | tf_op jit(solution)/shard_map/ppermute | solution.py:18
  174.3 8.2 %collective-permute-start.48 = (f32[4,18,1,128]{3,2,1,0:T(1,128)S(1)}, f32[4,18,1,128]{3,2,1,0:T(1,128)S(1)}, u32[]{:S(2)}, u32[]{:S(2)}) collective-permute-start(f32[4,18,1,128]{3,2,1,0:T(1,128)S(1)} %get-tuple-element.45), channel_id=1, source_target_pairs={{1,0},{2,1},{3,2},{5,4},{6,5},{7,6},{9,8},{10,9},{11,10},{13,12},{... | collective-permute-start | bytes 110600 | tf_op jit(solution)/shard_map/ppermute | solution.py:20
  176.6 6.0 %collective-permute-start.49 = (f32[4,18,1,128]{3,2,1,0:T(1,128)S(1)}, f32[4,18,1,128]{3,2,1,0:T(1,128)S(1)}, u32[]{:S(2)}, u32[]{:S(2)}) collective-permute-start(f32[4,18,1,128]{3,2,1,0:T(1,128)S(1)} %get-tuple-element.44), channel_id=1, source_target_pairs={{0,1},{1,2},{2,3},{4,5},{5,6},{6,7},{8,9},{9,10},{10,11},{12,13},{... | collective-permute-start | bytes 110600 | tf_op jit(solution)/shard_map/ppermute | solution.py:18
  181.3 5.7 %collective-permute-start.45 = (f32[16,16,128]{2,1,0:T(8,128)S(1)}, f32[16,16,128]{2,1,0:T(8,128)S(1)}, u32[]{:S(2)}, u32[]{:S(2)}) collective-permute-start(f32[16,16,128]{2,1,0:T(8,128)S(1)} %fusion.86), channel_id=1, source_target_pairs={{0,16},{1,17},{2,18},{3,19},{4,20},{5,21},{6,22},{7,23},{8,24},{9,... | collective-permute-start | bytes 393224 | tf_op jit(solution)/shard_map/ppermute | solution.py:30
where the time goes:
time: 190 us; the launch traced here: 188 us
  starting transfers between devices  115 us (61%)
  waiting for transfers between devices  58.5 us (31%)
  other arithmetic  9.12 us (5%)
  local copies, waits for them, and re-layouts  3.62 us (2%)
    ppermute x20, starting transfers between devices, padded_2(): lax.ppermute(tail, axis, [(i, (i + 1) % count) for i in range(ends)])  59 us
    ppermute x20, starting transfers between devices, padded_2(): lax.ppermute(head, axis, [((i + 1) % count, i) for i in range(ends)])  45.3 us
    ppermute x20, waiting for transfers between devices, padded_2(): lax.ppermute(tail, axis, [(i, (i + 1) % count) for i in range(ends)])  27.3 us
    ppermute x9, waiting for transfers between devices, shifted(): return lax.ppermute(value, axis, pairs)  26.6 us
    ppermute x9, starting transfers between devices, shifted(): return lax.ppermute(value, axis, pairs)  11 us
    ppermute x1, waiting for transfers between devices, partner_2(): lax.ppermute(value, axis, [(i, i ^ 1 << stride) for i in range(lax.axis_s...  4.52 us
    concatenate x18, other arithmetic, padded_2(): jnp.concatenate([lax.ppermute(tail, axis, [(i, (i + 1) % count) for i in...  4.16 us
  transfers between devices with their start and end apart: 50, of which 18 were waited for; matrix products, arithmetic and copies ran while one was open for 4% of the time, Pallas kernels for 0%

commit v1 on v0

v1 whole, which is shorter than its diff:
```python
import functools

import jax
import jax.numpy as jnp
from jax import lax
from jax.experimental import pallas as pl
from jax.experimental.pallas import tpu as pltpu
from jax.sharding import PartitionSpec as P

relax_weight = 0.8
keep_weight = 1.0 - relax_weight
MESH = pl.DeviceIdType.MESH

KAPPA, INIT, FIRST, ERR1, ERR2, ERR3, FIX2, FIX1, SUM0, SOL = range(10)
P_INIT, P_FIRST, P_ERR1, P_ERR2, P_FIX1, P_SUM0, P_SOL = range(7)
XLO, XHI, YLO, YHI = range(4)


def kernel(n_tm, n_sx, n_sy, unroll, hs_hbm, k_hbm, in_hbm, sol_hbm, res_hbm, *scratch):
    fields = scratch[:10]
    yrecv = scratch[10:20]
    ysend = scratch[20:30]
    (hs, res, before, second, rhs1, rhs2, rhs3, mine, theirs, chain,
     face, coupling, factor, send_sem, recv_sem, tsend, trecv,
     qsend, qrecv, csend, crecv, local) = scratch[30:]
    steps, nx, ny, nz = hs.shape
    tm, sx, sy = lax.axis_index("tm"), lax.axis_index("sx"), lax.axis_index("sy")
    has = (sx > 0, sx < n_sx - 1, sy > 0, sy < n_sy - 1)
    partner = tm + 1 - 2 * lax.rem(tm, 2)
    even = lax.rem(tm, 2) == 0

    loads = [
        pltpu.make_async_copy(k_hbm, fields[KAPPA].at[0, pl.ds(1, nx)], local.at[0]),
        pltpu.make_async_copy(in_hbm, fields[INIT].at[:, pl.ds(1, nx)], local.at[1]),
        pltpu.make_async_copy(hs_hbm, hs, local.at[2]),
    ]
    for load in loads:
        load.start()

    barrier = pltpu.get_barrier_semaphore()
    greet = [
        (has[XLO], {"sx": sx - 1}), (has[XHI], {"sx": sx + 1}),
        (has[YLO], {"sy": sy - 1}), (has[YHI], {"sy": sy + 1}),
        (tm > 0, {"tm": tm - 1}), (tm < n_tm - 1, {"tm": tm + 1}),
    ]
    if n_tm > 2:
        greet += [(tm > 1, {"tm": tm - 2}), (tm < n_tm - 2, {"tm": tm + 2})]
    count = jnp.int32(0)
    for there, device in greet:
        count = count + jnp.where(there, 1, 0)

        @pl.when(there)
        def _(device=device):
            pl.semaphore_signal(barrier, inc=1, device_id=device, device_id_type=MESH)

    pl.semaphore_wait(barrier, count)

    def face_copy(i, side):
        field = fields[i]
        if side == XLO:
            if i == INIT:
                src = in_hbm.at[:, pl.ds(0, 1)]
            elif i == KAPPA:
                src = k_hbm.at[pl.ds(0, 1)]
            else:
                src = field.at[:, pl.ds(1, 1)]
            dst, device = field.at[:, pl.ds(nx + 1, 1)], {"sx": sx - 1}
        elif side == XHI:
            if i == INIT:
                src = in_hbm.at[:, pl.ds(nx - 1, 1)]
            elif i == KAPPA:
                src = k_hbm.at[pl.ds(nx - 1, 1)]
            else:
                src = field.at[:, pl.ds(nx, 1)]
            dst, device = field.at[:, pl.ds(0, 1)], {"sx": sx + 1}
        elif side == YLO:
            src, dst, device = ysend[i].at[0], yrecv[i].at[1], {"sy": sy - 1}
        else:
            src, dst, device = ysend[i].at[1], yrecv[i].at[0], {"sy": sy + 1}
        if i == KAPPA and side in (XLO, XHI):
            dst = field.at[0, pl.ds(nx + 1 if side == XLO else 0, 1)]
        return pltpu.make_async_remote_copy(
            src_ref=src, dst_ref=dst, send_sem=send_sem.at[i, side],
            recv_sem=recv_sem.at[i, side], device_id=device, device_id_type=MESH)

    def send_faces(i, sides=(XLO, XHI, YLO, YHI)):
        for side in sides:
            @pl.when(has[side])
            def _(side=side):
                face_copy(i, side).start()

    def wait_faces(i):
        for side in (XLO, XHI, YLO, YHI):
            @pl.when(has[side ^ 1])
            def _(side=side):
                face_copy(i, side).wait_recv()

    def last_copy(i, field):
        if i == P_INIT:
            src = in_hbm.at[steps - 1]
        else:
            src = field.at[field.shape[0] - 1, pl.ds(1, nx)]
        return pltpu.make_async_remote_copy(
            src_ref=src, dst_ref=before.at[i], send_sem=tsend.at[i], recv_sem=trecv.at[i],
            device_id={"tm": tm + 1}, device_id_type=MESH)

    lasts = (INIT, FIRST, ERR1, ERR2, FIX1, SUM0, SOL)

    def send_last(i):
        @pl.when(tm < n_tm - 1)
        def _():
            last_copy(i, fields[lasts[i]]).start()

    def wait_last(i):
        @pl.when(tm > 0)
        def _():
            last_copy(i, fields[lasts[i]]).wait_recv()

    send_faces(KAPPA, (XLO, XHI))
    send_faces(INIT, (XLO, XHI))
    send_last(P_INIT)

    def over_rows(body, by=unroll):
        def step(x, carry):
            body(x)
            return carry

        lax.fori_loop(0, nx, step, 0, unroll=by)

    def put_faces(i, t, x, value):
        ysend[i][0, t, pl.ds(x, 1), :] = value[0:1, :]
        ysend[i][1, t, pl.ds(x, 1), :] = value[ny - 1:ny, :]

    def put(i, t, x, value):
        fields[i][t, x + 1] = value
        put_faces(i, t, x, value)

    loads[0].wait()
    loads[1].wait()

    def pack(x):
        put_faces(KAPPA, 0, x, fields[KAPPA][0, x + 1])
        for t in range(steps):
            put_faces(INIT, t, x, fields[INIT][t, x + 1])

    over_rows(pack)
    send_faces(KAPPA, (YLO, YHI))
    send_faces(INIT, (YLO, YHI))

    @pl.when(sx == 0)
    def _():
        for i in range(10):
            for t in range(fields[i].shape[0]):
                fields[i][t, 0] = jnp.zeros((ny, nz), jnp.float32)

    @pl.when(sx == n_sx - 1)
    def _():
        for i in range(10):
            for t in range(fields[i].shape[0]):
                fields[i][t, nx + 1] = jnp.zeros((ny, nz), jnp.float32)

    @pl.when(sy == 0)
    def _():
        for i in range(10):
            yrecv[i][0] = jnp.zeros(yrecv[i].shape[1:], jnp.float32)

    @pl.when(sy == n_sy - 1)
    def _():
        for i in range(10):
            yrecv[i][1] = jnp.zeros(yrecv[i].shape[1:], jnp.float32)

    @pl.when(tm == 0)
    def _():
        def clear(x):
            for i in range(7):
                before[i, x] = jnp.zeros((ny, nz), jnp.float32)

        over_rows(clear, 1)

    row = lax.broadcasted_iota(jnp.int32, (ny, nz), 0)
    column = lax.broadcasted_iota(jnp.int32, (ny, nz), 1)

    def around(i, t, x):
        field = fields[i]
        here = field[t, x + 1]
        return here, (
            field[t, x + 2],
            field[t, x],
            jnp.where(row == ny - 1, yrecv[i][1, t, pl.ds(x, 1), :], pltpu.roll(here, ny - 1, 0)),
            jnp.where(row == 0, yrecv[i][0, t, pl.ds(x, 1), :], pltpu.roll(here, 1, 0)),
            pltpu.roll(here, nz - 1, 1),
            pltpu.roll(here, 1, 1),
        )

    def beside(i, t, x, g):
        here, sides = around(i, t, x)
        terms = [g[j] * sides[j] for j in range(6)]
        return here, (terms[0] + terms[1]) + (terms[2] + terms[3]) + (terms[4] + terms[5])

    def faces_at(x):
        return [face[j, x] for j in range(6)]

    wait_faces(KAPPA)

    def coefficients(x):
        here, sides = around(KAPPA, 0, x)
        sides = list(sides)
        sides[4] = jnp.where(column == nz - 1, 0.0, sides[4])
        sides[5] = jnp.where(column == 0, 0.0, sides[5])
        g = [0.5 * (here + side) for side in sides]
        total = (g[0] + g[1]) + (g[2] + g[3]) + (g[4] + g[5])
        coupling[x] = total
        g[4] = jnp.where(column == nz - 1, 0.0, g[4])
        g[5] = jnp.where(column == 0, 0.0, g[5])
        for j in range(6):
            face[j, x] = g[j]
        for level in range(4):
            factor[level, x] = relax_weight / (1.0 + (2.0 ** level) * total)

    over_rows(coefficients)
    loads[2].wait()
    wait_faces(INIT)
    wait_last(P_INIT)

    def sweep_first(x):
        g, f = faces_at(x), factor[0, x]
        running = before[P_INIT, x]
        for t in range(steps):
            here, near = beside(INIT, t, x, g)
            running = keep_weight * here + f * (hs[t, x] + near + running)
            put(FIRST, t, x, running)

    over_rows(sweep_first)
    send_faces(FIRST)
    send_last(P_FIRST)
    wait_faces(FIRST)
    wait_last(P_FIRST)

    def down_one(x):
        g, diagonal, f = faces_at(x), 1.0 + coupling[x], factor[1, x]
        earlier = before[P_FIRST, x]
        running = None
        for m in range(steps // 2):
            total = None
            for t in (2 * m, 2 * m + 1):
                here, near = beside(FIRST, t, x, g)
                value = hs[t, x] + earlier - (diagonal * here - near)
                total = value if total is None else total + value
                earlier = here
            rhs1[m, x] = total
            running = f * total if running is None else f * (total + running)
            put(ERR1, m, x, running)

    over_rows(down_one)
    send_faces(ERR1)
    send_last(P_ERR1)
    wait_faces(ERR1)
    wait_last(P_ERR1)

    def down_two(x):
        g, diagonal, f = faces_at(x), 1.0 + 2.0 * coupling[x], factor[2, x]
        earlier = before[P_ERR1, x]
        total = None
        for t in range(2):
            here, near = beside(ERR1, t, x, g)
            value = rhs1[t, x] + earlier - (diagonal * here - 2.0 * near)
            total = value if total is None else total + value
            earlier = here
        rhs2[x] = total
        put(ERR2, 0, x, f * total)

    over_rows(down_two)
    send_faces(ERR2)
    send_last(P_ERR2)
    wait_faces(ERR2)
    if n_tm > 2:
        wait_last(P_ERR2)

    def down_three(x):
        g, diagonal = faces_at(x), 1.0 + 4.0 * coupling[x]
        here, near = beside(ERR2, 0, x, g)
        earlier = here + before[P_ERR2, x] if n_tm > 2 else here
        mine[x] = rhs2[x] + jnp.where(even, earlier, 0.0) - (diagonal * here - 4.0 * near)

    over_rows(down_three)
    swap = pltpu.make_async_remote_copy(
        src_ref=mine, dst_ref=theirs, send_sem=qsend, recv_sem=qrecv,
        device_id={"tm": partner}, device_id_type=MESH)
    swap.start()
    swap.wait_recv()

    def chain_copy(i, field):
        src = field.at[0, pl.ds(1, nx)] if i == 0 else second
        return pltpu.make_async_remote_copy(
            src_ref=src, dst_ref=chain.at[i], send_sem=csend.at[i],
            recv_sem=crecv.at[i], device_id={"tm": tm + 2}, device_id_type=MESH)

    def chain_wait(i):
        if n_tm > 2:
            @pl.when(tm > 1)
            def _():
                chain_copy(i, fields[ERR3]).wait_recv()

            @pl.when(tm < 2)
            def _():
                def clear(x):
                    chain[i, x] = jnp.zeros((ny, nz), jnp.float32)

                over_rows(clear, 1)

    def chain_send(i):
        if n_tm > 2:
            @pl.when(tm < n_tm - 2)
            def _():
                chain_copy(i, fields[ERR3]).start()

    chain_wait(0)

    def coarse_one(x):
        total = mine[x] + theirs[x]
        rhs3[x] = total
        if n_tm > 2:
            total = total + chain[0, x]
        put(ERR3, 0, x, factor[3, x] * total)

    over_rows(coarse_one)
    send_faces(ERR3)
    chain_send(0)
    wait_faces(ERR3)
    if n_tm == 2:
        wait_last(P_ERR2)
    chain_wait(1)

    def coarse_two(x):
        here, near = beside(ERR3, 0, x, faces_at(x))
        total = rhs3[x] + 8.0 * near
        if n_tm > 2:
            total = total + chain[1, x]
        value = keep_weight * here + factor[3, x] * total
        if n_tm > 2:
            second[x] = value
            earlier = jnp.where(even, chain[1, x], value)
        else:
            earlier = jnp.where(even, 0.0, value)
        mine_next[x] = before[P_ERR2, x] + earlier
        put(FIX2, 0, x, fields[ERR2][0, x + 1] + value)

    mine_next = res.at[0]
    over_rows(coarse_two)
    send_faces(FIX2)
    chain_send(1)
    wait_faces(FIX2)

    def up_two(x):
        here, near = beside(FIX2, 0, x, faces_at(x))
        value = keep_weight * here + factor[2, x] * (rhs2[x] + 4.0 * near + mine_next[x])
        for m in range(2):
            put(FIX1, m, x, fields[ERR1][m, x + 1] + value)

    over_rows(up_two)
    send_faces(FIX1)
    send_last(P_FIX1)
    wait_faces(FIX1)
    wait_last(P_FIX1)

    def up_one(x):
        g, f = faces_at(x), factor[1, x]
        running = before[P_FIX1, x]
        for m in range(2):
            here, near = beside(FIX1, m, x, g)
            running = keep_weight * here + f * (rhs1[m, x] + 2.0 * near + running)
            for t in (2 * m, 2 * m + 1):
                put(SUM0, t, x, fields[FIRST][t, x + 1] + running)

    over_rows(up_one)
    send_faces(SUM0)
    send_last(P_SUM0)
    wait_faces(SUM0)
    wait_last(P_SUM0)

    def up_zero(x):
        g, f = faces_at(x), factor[0, x]
        running = before[P_SUM0, x]
        for t in range(steps):
            here, near = beside(SUM0, t, x, g)
            running = keep_weight * here + f * (hs[t, x] + near + running)
            put(SOL, t, x, running)

    over_rows(up_zero)
    send_faces(SOL)
    send_last(P_SOL)
    out_one = pltpu.make_async_copy(fields[SOL].at[:, pl.ds(1, nx)], sol_hbm, local.at[3])
    out_one.start()
    wait_faces(SOL)
    wait_last(P_SOL)

    def last_defect(x):
        g, diagonal = faces_at(x), 1.0 + coupling[x]
        earlier = before[P_SOL, x]
        for t in range(steps):
            here, near = beside(SOL, t, x, g)
            res[t, x] = hs[t, x] + earlier - (diagonal * here - near)
            earlier = here

    over_rows(last_defect)
    out_two = pltpu.make_async_copy(res, res_hbm, local.at[4])
    out_two.start()

    for i in range(10):
        for side in (XLO, XHI, YLO, YHI):
            @pl.when(has[side])
            def _(i=i, side=side):
                face_copy(i, side).wait_send()

    @pl.when(tm < n_tm - 1)
    def _():
        for i in range(7):
            last_copy(i, fields[lasts[i]]).wait_send()

    swap.wait_send()
    if n_tm > 2:
        @pl.when(tm < n_tm - 2)
        def _():
            for i in range(2):
                chain_copy(i, fields[ERR3]).wait_send()

    out_one.wait()
    out_two.wait()


def solution(mesh):
    n_tm, n_sx, n_sy = (mesh.shape[axis] for axis in ("tm", "sx", "sy"))
    f32 = jnp.float32

    def per_device(heat_source, conductivity, initial_iterate):
        steps, nx, ny, nz = heat_source.shape
        depth = (1, steps, steps, steps // 2, 1, 1, 1, steps // 2, steps, steps)
        scratch = [pltpu.VMEM((d, nx + 2, ny, nz), f32) for d in depth]
        scratch += [pltpu.VMEM((2, d, nx, nz), f32) for d in depth] * 2
        cells = (nx, ny, nz)
        dma = pltpu.SemaphoreType.DMA
        scratch += [
            pltpu.VMEM((steps,) + cells, f32),
            pltpu.VMEM((steps,) + cells, f32),
            pltpu.VMEM((7,) + cells, f32),
            pltpu.VMEM(cells, f32),
            pltpu.VMEM((steps // 2,) + cells, f32),
            pltpu.VMEM(cells, f32),
            pltpu.VMEM(cells, f32),
            pltpu.VMEM(cells, f32),
            pltpu.VMEM(cells, f32),
            pltpu.VMEM((2,) + cells, f32),
            pltpu.VMEM((6,) + cells, f32),
            pltpu.VMEM(cells, f32),
            pltpu.VMEM((4,) + cells, f32),
            dma((10, 4)), dma((10, 4)), dma((7,)), dma((7,)),
            dma, dma, dma((2,)), dma((2,)), dma((5,)),
        ]
        field = jax.ShapeDtypeStruct(heat_source.shape, f32)
        return pl.pallas_call(
            functools.partial(kernel, n_tm, n_sx, n_sy, 2),
            out_shape=(field, field),
            in_specs=[pl.BlockSpec(memory_space=pl.ANY)] * 3,
            out_specs=(pl.BlockSpec(memory_space=pl.ANY),) * 2,
            scratch_shapes=scratch,
            compiler_params=pltpu.CompilerParams(
                collective_id=0, has_side_effects=True, vmem_limit_bytes=40 * 2 ** 20
            ),
            name="vcycle",
        )(heat_source, conductivity, initial_iterate)

    placed = (P("tm", "sx", "sy", None), P("sx", "sy", None), P("tm", "sx", "sy", None))
    return jax.shard_map(
        per_device,
        mesh=mesh,
        in_specs=placed,
        out_specs=(P("tm", "sx", "sy", None), P("tm", "sx", "sy", None)),
        check_vma=False,
    )
```

time: 190 us -> 50.7 us (0.27)
  the two profiles are of different devices: /device:TPU:27 before, /device:TPU:0 now
where the time goes in v1:
time: 50.7 us; the launch traced here: 50.4 us
  Pallas kernels  45.2 us (89%)
  local copies, waits for them, and re-layouts  4.57 us (9%)
  between operations  0.65 us (1%)
    pallas_call x1, Pallas kernels, per_device(): pl.pallas_call(functools.partial(kernel, n_tm, n_sx, n_sy, 2), out_shape=...  45.2 us
    unnamed x8, local copies, waits for them, and re-layouts  4.57 us

profile of v1, /device:TPU:0, one launch (start us, length us, event | category | flops | bytes accessed | tf_op | source)
XLA Modules:
  0.0 50.4 jit_solution(5171373607521473903)
XLA Ops:
  0.6 0.0 copy-start
  0.6 1.0 %copy-done = f32[4,16,16,128]{3,2,1,0:T(8,128)S(1)} copy-done((f32[4,16,16,128]{3,2,1,0:T(8,128)S(1)}, f32[4,16,16,128]{3,2,1,0:T(8,128)}, u32[]{:S(2)}) %copy-start) | copy-done | bytes 524312
  1.7 0.0 copy-start.1
  1.7 1.0 %copy-done.1 = f32[4,16,16,128]{3,2,1,0:T(8,128)S(1)} copy-done((f32[4,16,16,128]{3,2,1,0:T(8,128)S(1)}, f32[4,16,16,128]{3,2,1,0:T(8,128)}, u32[]{:S(2)}) %copy-start.1) | copy-done | bytes 524312
  2.7 0.0 copy-start.2
  2.7 0.9 %copy-done.2 = f32[16,16,128]{2,1,0:T(8,128)S(1)} copy-done((f32[16,16,128]{2,1,0:T(8,128)S(1)}, f32[16,16,128]{2,1,0:T(8,128)}, u32[]{:S(2)}) %copy-start.2) | copy-done | bytes 131096
  3.6 45.2 %vcycle.1 = (f32[4,16,16,128]{3,2,1,0:T(8,128)S(1)}, f32[4,16,16,128]{3,2,1,0:T(8,128)S(1)}) custom-call(f32[4,16,16,128]{3,2,1,0:T(8,128)S(1)} %copy-done, f32[16,16,128]{2,1,0:T(8,128)S(1)} %copy-done.2, f32[4,16,16,128]{3,2,1,0:T(8,128)S(1)} %copy-done.1), custom_call_target="tpu_custom_call" | custom-call | tf_op jit(solution)/shard_map/vcycle/pallas_call | solution.py:460
  48.9 0.8 %copy.7 = f32[4,16,16,128]{3,2,1,0:T(8,128)} copy(f32[4,16,16,128]{3,2,1,0:T(8,128)S(1)} %get-tuple-element.4) | data formatting | bytes 1048576
  49.6 0.8 %copy.8 = f32[4,16,16,128]{3,2,1,0:T(8,128)} copy(f32[4,16,16,128]{3,2,1,0:T(8,128)S(1)} %get-tuple-element.5) | data formatting | bytes 1048576
Async XLA Ops:
  0.6 1.0 %copy-start = (f32[4,16,16,128]{3,2,1,0:T(8,128)S(1)}, f32[4,16,16,128]{3,2,1,0:T(8,128)}, u32[]{:S(2)}) copy-start(f32[4,16,16,128]{3,2,1,0:T(8,128)} %hs_hbm.1) | copy-start | bytes 1572868
  1.7 1.0 %copy-start.1 = (f32[4,16,16,128]{3,2,1,0:T(8,128)S(1)}, f32[4,16,16,128]{3,2,1,0:T(8,128)}, u32[]{:S(2)}) copy-start(f32[4,16,16,128]{3,2,1,0:T(8,128)} %in_hbm.1) | copy-start | bytes 1572868
  2.7 0.9 %copy-start.2 = (f32[16,16,128]{2,1,0:T(8,128)S(1)}, f32[16,16,128]{2,1,0:T(8,128)}, u32[]{:S(2)}) copy-start(f32[16,16,128]{2,1,0:T(8,128)} %k_hbm.1) | copy-start | bytes 393220

commit v2 on v1

--- a/solution.py
+++ b/solution.py
@@ -458,13 +458,13 @@
         ]
         field = jax.ShapeDtypeStruct(heat_source.shape, f32)
         return pl.pallas_call(
-            functools.partial(kernel, n_tm, n_sx, n_sy, 2),
+            functools.partial(kernel, n_tm, n_sx, n_sy, 8),
             out_shape=(field, field),
-            in_specs=[pl.BlockSpec(memory_space=pl.ANY)] * 3,
-            out_specs=(pl.BlockSpec(memory_space=pl.ANY),) * 2,
+            in_specs=[pl.BlockSpec(memory_space=pltpu.HBM)] * 3,
+            out_specs=(pl.BlockSpec(memory_space=pltpu.HBM),) * 2,
             scratch_shapes=scratch,
             compiler_params=pltpu.CompilerParams(
-                collective_id=0, has_side_effects=True, vmem_limit_bytes=40 * 2 ** 20
+                collective_id=0, has_side_effects=True, vmem_limit_bytes=67043328
             ),
             name="vcycle",
         )(heat_source, conductivity, initial_iterate)

time: 50.7 us -> 45.6 us (0.90)
  Pallas kernels: 45.2 us -> 42.1 us
  local copies, waits for them, and re-layouts: 4.57 us -> 2.72 us
    pallas_call x1, Pallas kernels: 45.2 us -> 42.1 us  [per_device(): pl.pallas_call(functools.partial(kernel, n_tm, n_sx, n_sy, 8), out_shape=...]
    unnamed x8 -> x4, local copies, waits for them, and re-layouts: 4.57 us -> 2.72 us
where the time goes in v2:
time: 45.6 us; the launch traced here: 45.5 us
  Pallas kernels  42.1 us (92%)
  local copies, waits for them, and re-layouts  2.72 us (6%)
  between operations  0.65 us (1%)
    pallas_call x1, Pallas kernels, per_device(): pl.pallas_call(functools.partial(kernel, n_tm, n_sx, n_sy, 8), out_shape=...  42.1 us
    unnamed x4, local copies, waits for them, and re-layouts  2.72 us

profile of v2, /device:TPU:0, one launch (start us, length us, event | category | flops | bytes accessed | tf_op | source)
XLA Modules:
  0.0 45.5 jit_solution(15711961536732805128)
XLA Ops:
  0.6 42.1 %vcycle.1 = (f32[4,16,16,128]{3,2,1,0:T(8,128)}, f32[4,16,16,128]{3,2,1,0:T(8,128)}) custom-call(f32[4,16,16,128]{3,2,1,0:T(8,128)} %hs_hbm.1, f32[16,16,128]{2,1,0:T(8,128)} %k_hbm.1, f32[4,16,16,128]{3,2,1,0:T(8,128)} %in_hbm.1), custom_call_target="tpu_custom_call" | custom-call | tf_op jit(solution)/shard_map/vcycle/pallas_call | solution.py:460
  42.8 0.0 copy-start
  42.8 1.9 %copy.7 = f32[4,16,16,128]{3,2,1,0:T(8,128)} copy(f32[4,16,16,128]{3,2,1,0:T(8,128)} %get-tuple-element.4) | data formatting | bytes 1048576
  44.7 0.0 copy-done
  44.7 0.8 %copy.8 = f32[4,16,16,128]{3,2,1,0:T(8,128)} copy(f32[4,16,16,128]{3,2,1,0:T(8,128)S(1)} %copy-done) | data formatting | bytes 1048576
Async XLA Ops:
  42.8 1.9 %copy-start = (f32[4,16,16,128]{3,2,1,0:T(8,128)S(1)}, f32[4,16,16,128]{3,2,1,0:T(8,128)}, u32[]{:S(2)}) copy-start(f32[4,16,16,128]{3,2,1,0:T(8,128)} %get-tuple-element.5) | copy-start | bytes 1572868

commit v3 on v2

--- a/solution.py
+++ b/solution.py
@@ -11,18 +11,19 @@
 keep_weight = 1.0 - relax_weight
 MESH = pl.DeviceIdType.MESH
 
-KAPPA, INIT, FIRST, ERR1, ERR2, ERR3, FIX2, FIX1, SUM0, SOL = range(10)
+KAPPA, INIT, FIRST, ERR1, ERR2, ERR3, FIX2, FIX1, SUM0, SOL, PART, PAIR = range(12)
+FIELDS = 12
 P_INIT, P_FIRST, P_ERR1, P_ERR2, P_FIX1, P_SUM0, P_SOL = range(7)
 XLO, XHI, YLO, YHI = range(4)
 
 
-def kernel(n_tm, n_sx, n_sy, unroll, hs_hbm, k_hbm, in_hbm, sol_hbm, res_hbm, *scratch):
-    fields = scratch[:10]
-    yrecv = scratch[10:20]
-    ysend = scratch[20:30]
+def kernel(n_tm, n_sx, n_sy, hs_hbm, k_hbm, in_hbm, sol_hbm, res_hbm, *scratch):
+    fields = scratch[:FIELDS]
+    yrecv = scratch[FIELDS:2 * FIELDS]
+    ysend = scratch[2 * FIELDS:3 * FIELDS]
     (hs, res, before, second, rhs1, rhs2, rhs3, mine, theirs, chain,
      face, coupling, factor, send_sem, recv_sem, tsend, trecv,
-     qsend, qrecv, csend, crecv, local) = scratch[30:]
+     qsend, qrecv, csend, crecv, local) = scratch[3 * FIELDS:]
     steps, nx, ny, nz = hs.shape
     tm, sx, sy = lax.axis_index("tm"), lax.axis_index("sx"), lax.axis_index("sy")
     has = (sx > 0, sx < n_sx - 1, sy > 0, sy < n_sy - 1)
@@ -43,6 +44,11 @@
         (has[YLO], {"sy": sy - 1}), (has[YHI], {"sy": sy + 1}),
         (tm > 0, {"tm": tm - 1}), (tm < n_tm - 1, {"tm": tm + 1}),
     ]
+    if n_tm == 2:
+        greet += [
+            (has[XLO], {"tm": partner, "sx": sx - 1}), (has[XHI], {"tm": partner, "sx": sx + 1}),
+            (has[YLO], {"tm": partner, "sy": sy - 1}), (has[YHI], {"tm": partner, "sy": sy + 1}),
+        ]
     if n_tm > 2:
         greet += [(tm > 1, {"tm": tm - 2}), (tm < n_tm - 2, {"tm": tm + 2})]
     count = jnp.int32(0)
@@ -55,8 +61,10 @@
 
     pl.semaphore_wait(barrier, count)
 
-    def face_copy(i, side):
+    def face_copy(i, side, pair=False):
         field = fields[i]
+        to = PAIR if pair else i
+        land = fields[to]
         if side == XLO:
             if i == INIT:
                 src = in_hbm.at[:, pl.ds(0, 1)]
@@ -64,7 +72,7 @@
                 src = k_hbm.at[pl.ds(0, 1)]
             else:
                 src = field.at[:, pl.ds(1, 1)]
-            dst, device = field.at[:, pl.ds(nx + 1, 1)], {"sx": sx - 1}
+            dst, device = land.at[:, pl.ds(nx + 1, 1)], {"sx": sx - 1}
         elif side == XHI:
             if i == INIT:
                 src = in_hbm.at[:, pl.ds(nx - 1, 1)]
@@ -72,60 +80,85 @@
                 src = k_hbm.at[pl.ds(nx - 1, 1)]
             else:
                 src = field.at[:, pl.ds(nx, 1)]
-            dst, device = field.at[:, pl.ds(0, 1)], {"sx": sx + 1}
+            dst, device = land.at[:, pl.ds(0, 1)], {"sx": sx + 1}
         elif side == YLO:
-            src, dst, device = ysend[i].at[0], yrecv[i].at[1], {"sy": sy - 1}
+            src, dst, device = ysend[i].at[0], yrecv[to].at[1], {"sy": sy - 1}
         else:
-            src, dst, device = ysend[i].at[1], yrecv[i].at[0], {"sy": sy + 1}
+            src, dst, device = ysend[i].at[1], yrecv[to].at[0], {"sy": sy + 1}
         if i == KAPPA and side in (XLO, XHI):
             dst = field.at[0, pl.ds(nx + 1 if side == XLO else 0, 1)]
+        if pair:
+            device["tm"] = partner
         return pltpu.make_async_remote_copy(
-            src_ref=src, dst_ref=dst, send_sem=send_sem.at[i, side],
-            recv_sem=recv_sem.at[i, side], device_id=device, device_id_type=MESH)
-
-    def send_faces(i, sides=(XLO, XHI, YLO, YHI)):
+            src_ref=src, dst_ref=dst, send_sem=send_sem.at[to, side],
+            recv_sem=recv_sem.at[to, side], device_id=device, device_id_type=MESH)
+
+    def send_faces(i, sides, pair=False):
         for side in sides:
             @pl.when(has[side])
             def _(side=side):
                 face_copy(i, side).start()
-
-    def wait_faces(i):
-        for side in (XLO, XHI, YLO, YHI):
+                if pair:
+                    face_copy(i, side, True).start()
+
+    def wait_faces(i, pair=False):
+        for side in (YLO, YHI, XLO, XHI):
             @pl.when(has[side ^ 1])
             def _(side=side):
                 face_copy(i, side).wait_recv()
-
-    def last_copy(i, field):
+                if pair:
+                    face_copy(i, side, True).wait_recv()
+
+    half = nx // 2
+    halves = (pl.ds(0, half), pl.ds(half, nx - half))
+
+    def last_copy(i, part):
+        field = fields[lasts[i]]
         if i == P_INIT:
-            src = in_hbm.at[steps - 1]
+            src = in_hbm.at[steps - 1, halves[part]]
         else:
-            src = field.at[field.shape[0] - 1, pl.ds(1, nx)]
+            src = field.at[field.shape[0] - 1, (pl.ds(1, half), pl.ds(1 + half, nx - half))[part]]
         return pltpu.make_async_remote_copy(
-            src_ref=src, dst_ref=before.at[i], send_sem=tsend.at[i], recv_sem=trecv.at[i],
+            src_ref=src, dst_ref=before.at[i, halves[part]],
+            send_sem=tsend.at[i, part], recv_sem=trecv.at[i, part],
             device_id={"tm": tm + 1}, device_id_type=MESH)
 
     lasts = (INIT, FIRST, ERR1, ERR2, FIX1, SUM0, SOL)
 
-    def send_last(i):
+    def send_last(i, part):
         @pl.when(tm < n_tm - 1)
         def _():
-            last_copy(i, fields[lasts[i]]).start()
+            last_copy(i, part).start()
 
     def wait_last(i):
         @pl.when(tm > 0)
         def _():
-            last_copy(i, fields[lasts[i]]).wait_recv()
+            for part in range(2):
+                last_copy(i, part).wait_recv()
 
     send_faces(KAPPA, (XLO, XHI))
     send_faces(INIT, (XLO, XHI))
-    send_last(P_INIT)
-
-    def over_rows(body, by=unroll):
+    send_last(P_INIT, 0)
+    send_last(P_INIT, 1)
+
+    def over_rows(body, by=8, start=0, stop=nx):
         def step(x, carry):
             body(x)
             return carry
 
-        lax.fori_loop(0, nx, step, 0, unroll=by)
+        lax.fori_loop(start, stop, step, 0, unroll=by)
+
+    def phase(body, i, send_part=None, pair=False):
+        body(0)
+        body(nx - 1)
+        send_faces(i, (XLO, XHI), pair)
+        over_rows(body, half - 1, 1, half)
+        if send_part is not None:
+            send_part(0)
+        over_rows(body, half - 1, half, nx - 1)
+        send_faces(i, (YLO, YHI), pair)
+        if send_part is not None:
+            send_part(1)
 
     def put_faces(i, t, x, value):
         ysend[i][0, t, pl.ds(x, 1), :] = value[0:1, :]
@@ -149,24 +182,24 @@
 
     @pl.when(sx == 0)
     def _():
-        for i in range(10):
+        for i in range(FIELDS):
             for t in range(fields[i].shape[0]):
                 fields[i][t, 0] = jnp.zeros((ny, nz), jnp.float32)
 
     @pl.when(sx == n_sx - 1)
     def _():
-        for i in range(10):
+        for i in range(FIELDS):
             for t in range(fields[i].shape[0]):
                 fields[i][t, nx + 1] = jnp.zeros((ny, nz), jnp.float32)
 
     @pl.when(sy == 0)
     def _():
-        for i in range(10):
+        for i in range(FIELDS):
             yrecv[i][0] = jnp.zeros(yrecv[i].shape[1:], jnp.float32)
 
     @pl.when(sy == n_sy - 1)
     def _():
-        for i in range(10):
+        for i in range(FIELDS):
             yrecv[i][1] = jnp.zeros(yrecv[i].shape[1:], jnp.float32)
 
     @pl.when(tm == 0)
@@ -230,9 +263,7 @@
             running = keep_weight * here + f * (hs[t, x] + near + running)
             put(FIRST, t, x, running)
 
-    over_rows(sweep_first)
-    send_faces(FIRST)
-    send_last(P_FIRST)
+    phase(sweep_first, FIRST, functools.partial(send_last, P_FIRST))
     wait_faces(FIRST)
     wait_last(P_FIRST)
 
@@ -251,9 +282,7 @@
             running = f * total if running is None else f * (total + running)
             put(ERR1, m, x, running)
 
-    over_rows(down_one)
-    send_faces(ERR1)
-    send_last(P_ERR1)
+    phase(down_one, ERR1, functools.partial(send_last, P_ERR1))
     wait_faces(ERR1)
     wait_last(P_ERR1)
 
@@ -269,9 +298,7 @@
         rhs2[x] = total
         put(ERR2, 0, x, f * total)
 
-    over_rows(down_two)
-    send_faces(ERR2)
-    send_last(P_ERR2)
+    phase(down_two, ERR2, functools.partial(send_last, P_ERR2))
     wait_faces(ERR2)
     if n_tm > 2:
         wait_last(P_ERR2)
@@ -280,14 +307,25 @@
         g, diagonal = faces_at(x), 1.0 + 4.0 * coupling[x]
         here, near = beside(ERR2, 0, x, g)
         earlier = here + before[P_ERR2, x] if n_tm > 2 else here
-        mine[x] = rhs2[x] + jnp.where(even, earlier, 0.0) - (diagonal * here - 4.0 * near)
-
-    over_rows(down_three)
-    swap = pltpu.make_async_remote_copy(
-        src_ref=mine, dst_ref=theirs, send_sem=qsend, recv_sem=qrecv,
-        device_id={"tm": partner}, device_id_type=MESH)
-    swap.start()
-    swap.wait_recv()
+        value = rhs2[x] + jnp.where(even, earlier, 0.0) - (diagonal * here - 4.0 * near)
+        mine[x] = value
+        if n_tm == 2:
+            put(PART, 0, x, factor[3, x] * value)
+
+    def swap(part):
+        return pltpu.make_async_remote_copy(
+            src_ref=mine.at[halves[part]], dst_ref=theirs.at[halves[part]],
+            send_sem=qsend.at[part], recv_sem=qrecv.at[part],
+            device_id={"tm": partner}, device_id_type=MESH)
+
+    if n_tm == 2:
+        phase(down_three, PART, lambda part: swap(part).start(), True)
+    else:
+        over_rows(down_three)
+        swap(0).start()
+        swap(1).start()
+    swap(0).wait_recv()
+    swap(1).wait_recv()
 
     def chain_copy(i, field):
         src = field.at[0, pl.ds(1, nx)] if i == 0 else second
@@ -321,12 +359,23 @@
         rhs3[x] = total
         if n_tm > 2:
             total = total + chain[0, x]
-        put(ERR3, 0, x, factor[3, x] * total)
-
-    over_rows(coarse_one)
-    send_faces(ERR3)
-    chain_send(0)
-    wait_faces(ERR3)
+        value = factor[3, x] * total
+        if n_tm > 2:
+            put(ERR3, 0, x, value)
+        else:
+            fields[ERR3][0, x + 1] = value
+
+    if n_tm > 2:
+        phase(coarse_one, ERR3)
+        chain_send(0)
+        wait_faces(ERR3)
+    else:
+        over_rows(coarse_one)
+        wait_faces(PART, True)
+        for edge in (0, nx + 1):
+            fields[ERR3][0, edge] = fields[PART][0, edge] + fields[PAIR][0, edge]
+        for edge in range(2):
+            yrecv[ERR3][edge, 0] = yrecv[PART][edge, 0] + yrecv[PAIR][edge, 0]
     if n_tm == 2:
         wait_last(P_ERR2)
     chain_wait(1)
@@ -346,8 +395,7 @@
         put(FIX2, 0, x, fields[ERR2][0, x + 1] + value)
 
     mine_next = res.at[0]
-    over_rows(coarse_two)
-    send_faces(FIX2)
+    phase(coarse_two, FIX2)
     chain_send(1)
     wait_faces(FIX2)
 
@@ -357,9 +405,7 @@
         for m in range(2):
             put(FIX1, m, x, fields[ERR1][m, x + 1] + value)
 
-    over_rows(up_two)
-    send_faces(FIX1)
-    send_last(P_FIX1)
+    phase(up_two, FIX1, functools.partial(send_last, P_FIX1))
     wait_faces(FIX1)
     wait_last(P_FIX1)
 
@@ -372,9 +418,7 @@
             for t in (2 * m, 2 * m + 1):
                 put(SUM0, t, x, fields[FIRST][t, x + 1] + running)
 
-    over_rows(up_one)
-    send_faces(SUM0)
-    send_last(P_SUM0)
+    phase(up_one, SUM0, functools.partial(send_last, P_SUM0))
     wait_faces(SUM0)
     wait_last(P_SUM0)
 
@@ -386,9 +430,7 @@
             running = keep_weight * here + f * (hs[t, x] + near + running)
             put(SOL, t, x, running)
 
-    over_rows(up_zero)
-    send_faces(SOL)
-    send_last(P_SOL)
+    phase(up_zero, SOL, functools.partial(send_last, P_SOL))
     out_one = pltpu.make_async_copy(fields[SOL].at[:, pl.ds(1, nx)], sol_hbm, local.at[3])
     out_one.start()
     wait_faces(SOL)
@@ -406,18 +448,24 @@
     out_two = pltpu.make_async_copy(res, res_hbm, local.at[4])
     out_two.start()
 
-    for i in range(10):
+    for i in range(FIELDS):
+        if i == PAIR or i == (ERR3 if n_tm == 2 else PART):
+            continue
         for side in (XLO, XHI, YLO, YHI):
             @pl.when(has[side])
             def _(i=i, side=side):
                 face_copy(i, side).wait_send()
+                if i == PART:
+                    face_copy(i, side, True).wait_send()
 
     @pl.when(tm < n_tm - 1)
     def _():
         for i in range(7):
-            last_copy(i, fields[lasts[i]]).wait_send()
-
-    swap.wait_send()
+            for part in range(2):
+                last_copy(i, part).wait_send()
+
+    swap(0).wait_send()
+    swap(1).wait_send()
     if n_tm > 2:
         @pl.when(tm < n_tm - 2)
         def _():
@@ -434,7 +482,7 @@
 
     def per_device(heat_source, conductivity, initial_iterate):
         steps, nx, ny, nz = heat_source.shape
-        depth = (1, steps, steps, steps // 2, 1, 1, 1, steps // 2, steps, steps)
+        depth = (1, steps, steps, steps // 2, 1, 1, 1, steps // 2, steps, steps, 1, 1)
         scratch = [pltpu.VMEM((d, nx + 2, ny, nz), f32) for d in depth]
         scratch += [pltpu.VMEM((2, d, nx, nz), f32) for d in depth] * 2
         cells = (nx, ny, nz)
@@ -453,12 +501,12 @@
             pltpu.VMEM((6,) + cells, f32),
             pltpu.VMEM(cells, f32),
             pltpu.VMEM((4,) + cells, f32),
-            dma((10, 4)), dma((10, 4)), dma((7,)), dma((7,)),
-            dma, dma, dma((2,)), dma((2,)), dma((5,)),
+            dma((FIELDS, 4)), dma((FIELDS, 4)), dma((7, 2)), dma((7, 2)),
+            dma((2,)), dma((2,)), dma((2,)), dma((2,)), dma((5,)),
         ]
         field = jax.ShapeDtypeStruct(heat_source.shape, f32)
         return pl.pallas_call(
-            functools.partial(kernel, n_tm, n_sx, n_sy, 8),
+            functools.partial(kernel, n_tm, n_sx, n_sy),
             out_shape=(field, field),
             in_specs=[pl.BlockSpec(memory_space=pltpu.HBM)] * 3,
             out_specs=(pl.BlockSpec(memory_space=pltpu.HBM),) * 2,

time: 45.6 us -> 42.9 us (0.941)
  Pallas kernels: 42.1 us -> 39.1 us
    pallas_call x1, Pallas kernels: 42.1 us -> 39.1 us  [per_device(): pl.pallas_call(functools.partial(kernel, n_tm, n_sx, n_sy), out_shape=(fi...]
where the time goes in v3:
time: 42.9 us; the launch traced here: 42.5 us
  Pallas kernels  39.1 us (91%)
  local copies, waits for them, and re-layouts  2.72 us (6%)
  between operations  0.65 us (2%)
    pallas_call x1, Pallas kernels, per_device(): pl.pallas_call(functools.partial(kernel, n_tm, n_sx, n_sy), out_shape=(fi...  39.1 us
    unnamed x4, local copies, waits for them, and re-layouts  2.72 us

profile of v3, /device:TPU:0, one launch (start us, length us, event | category | flops | bytes accessed | tf_op | source)
XLA Modules:
  0.0 42.5 jit_solution(3299288472235741180)
XLA Ops:
  0.6 39.1 %vcycle.1 = (f32[4,16,16,128]{3,2,1,0:T(8,128)}, f32[4,16,16,128]{3,2,1,0:T(8,128)}) custom-call(f32[4,16,16,128]{3,2,1,0:T(8,128)} %hs_hbm.1, f32[16,16,128]{2,1,0:T(8,128)} %k_hbm.1, f32[4,16,16,128]{3,2,1,0:T(8,128)} %in_hbm.1), custom_call_target="tpu_custom_call" | custom-call | tf_op jit(solution)/shard_map/vcycle/pallas_call | solution.py:508
  39.8 0.0 copy-start
  39.8 1.9 %copy.7 = f32[4,16,16,128]{3,2,1,0:T(8,128)} copy(f32[4,16,16,128]{3,2,1,0:T(8,128)} %get-tuple-element.4) | data formatting | bytes 1048576
  41.7 0.0 copy-done
  41.7 0.8 %copy.8 = f32[4,16,16,128]{3,2,1,0:T(8,128)} copy(f32[4,16,16,128]{3,2,1,0:T(8,128)S(1)} %copy-done) | data formatting | bytes 1048576
Async XLA Ops:
  39.8 1.9 %copy-start = (f32[4,16,16,128]{3,2,1,0:T(8,128)S(1)}, f32[4,16,16,128]{3,2,1,0:T(8,128)}, u32[]{:S(2)}) copy-start(f32[4,16,16,128]{3,2,1,0:T(8,128)} %get-tuple-element.5) | copy-start | bytes 1572868

commit v4 on v3

--- a/solution.py
+++ b/solution.py
@@ -11,8 +11,8 @@
 keep_weight = 1.0 - relax_weight
 MESH = pl.DeviceIdType.MESH
 
-KAPPA, INIT, FIRST, ERR1, ERR2, ERR3, FIX2, FIX1, SUM0, SOL, PART, PAIR = range(12)
-FIELDS = 12
+KAPPA, INIT, FIRST, ERR1, ERR2, ERR3, FIX2, FIX1, SUM0, SOL, PART, PAIR, PART2, PAIR2 = range(14)
+FIELDS = 14
 P_INIT, P_FIRST, P_ERR1, P_ERR2, P_FIX1, P_SUM0, P_SOL = range(7)
 XLO, XHI, YLO, YHI = range(4)
 
@@ -63,7 +63,7 @@
 
     def face_copy(i, side, pair=False):
         field = fields[i]
-        to = PAIR if pair else i
+        to = i + 1 if pair else i
         land = fields[to]
         if side == XLO:
             if i == INIT:
@@ -105,9 +105,7 @@
         for side in (YLO, YHI, XLO, XHI):
             @pl.when(has[side ^ 1])
             def _(side=side):
-                face_copy(i, side).wait_recv()
-                if pair:
-                    face_copy(i, side, True).wait_recv()
+                face_copy(i, side, pair).wait_recv()
 
     half = nx // 2
     halves = (pl.ds(0, half), pl.ds(half, nx - half))
@@ -130,10 +128,10 @@
         def _():
             last_copy(i, part).start()
 
-    def wait_last(i):
+    def wait_last(i, parts=(0, 1)):
         @pl.when(tm > 0)
         def _():
-            for part in range(2):
+            for part in parts:
                 last_copy(i, part).wait_recv()
 
     send_faces(KAPPA, (XLO, XHI))
@@ -148,13 +146,22 @@
 
         lax.fori_loop(start, stop, step, 0, unroll=by)
 
-    def phase(body, i, send_part=None, pair=False):
+    def phase(body, i, send_part=None, pair=False, awaited=None):
+        if awaited is not None:
+            wait_last(awaited, (0,))
         body(0)
-        body(nx - 1)
-        send_faces(i, (XLO, XHI), pair)
+        if awaited is None:
+            body(nx - 1)
+            send_faces(i, (XLO, XHI), pair)
+        else:
+            send_faces(i, (XLO,), pair)
         over_rows(body, half - 1, 1, half)
         if send_part is not None:
             send_part(0)
+        if awaited is not None:
+            wait_last(awaited, (1,))
+            body(nx - 1)
+            send_faces(i, (XHI,), pair)
         over_rows(body, half - 1, half, nx - 1)
         send_faces(i, (YLO, YHI), pair)
         if send_part is not None:
@@ -253,7 +260,6 @@
     over_rows(coefficients)
     loads[2].wait()
     wait_faces(INIT)
-    wait_last(P_INIT)
 
     def sweep_first(x):
         g, f = faces_at(x), factor[0, x]
@@ -263,9 +269,8 @@
             running = keep_weight * here + f * (hs[t, x] + near + running)
             put(FIRST, t, x, running)
 
-    phase(sweep_first, FIRST, functools.partial(send_last, P_FIRST))
+    phase(sweep_first, FIRST, functools.partial(send_last, P_FIRST), awaited=P_INIT)
     wait_faces(FIRST)
-    wait_last(P_FIRST)
 
     def down_one(x):
         g, diagonal, f = faces_at(x), 1.0 + coupling[x], factor[1, x]
@@ -282,7 +287,7 @@
             running = f * total if running is None else f * (total + running)
             put(ERR1, m, x, running)
 
-    phase(down_one, ERR1, functools.partial(send_last, P_ERR1))
+    phase(down_one, ERR1, functools.partial(send_last, P_ERR1), awaited=P_FIRST)
     wait_faces(ERR1)
     wait_last(P_ERR1)
 
@@ -320,6 +325,13 @@
 
     if n_tm == 2:
         phase(down_three, PART, lambda part: swap(part).start(), True)
+        wait_faces(PART)
+
+        def part_two(x):
+            here, near = beside(PART, 0, x, faces_at(x))
+            put(PART2, 0, x, keep_weight * here + factor[3, x] * (mine[x] + 8.0 * near))
+
+        phase(part_two, PART2, None, True)
     else:
         over_rows(down_three)
         swap(0).start()
@@ -392,12 +404,27 @@
         else:
             earlier = jnp.where(even, 0.0, value)
         mine_next[x] = before[P_ERR2, x] + earlier
-        put(FIX2, 0, x, fields[ERR2][0, x + 1] + value)
+        value = fields[ERR2][0, x + 1] + value
+        if n_tm > 2:
+            put(FIX2, 0, x, value)
+        else:
+            fields[FIX2][0, x + 1] = value
 
     mine_next = res.at[0]
-    phase(coarse_two, FIX2)
-    chain_send(1)
-    wait_faces(FIX2)
+    if n_tm > 2:
+        phase(coarse_two, FIX2)
+        chain_send(1)
+        wait_faces(FIX2)
+    else:
+        over_rows(coarse_two)
+        wait_faces(PART2)
+        wait_faces(PART2, True)
+        for edge in (0, nx + 1):
+            fields[FIX2][0, edge] = fields[ERR2][0, edge] + (
+                fields[PART2][0, edge] + fields[PAIR2][0, edge])
+        for edge in range(2):
+            yrecv[FIX2][edge, 0] = yrecv[ERR2][edge, 0] + (
+                yrecv[PART2][edge, 0] + yrecv[PAIR2][edge, 0])
 
     def up_two(x):
         here, near = beside(FIX2, 0, x, faces_at(x))
@@ -407,7 +434,6 @@
 
     phase(up_two, FIX1, functools.partial(send_last, P_FIX1))
     wait_faces(FIX1)
-    wait_last(P_FIX1)
 
     def up_one(x):
         g, f = faces_at(x), factor[1, x]
@@ -418,7 +444,7 @@
             for t in (2 * m, 2 * m + 1):
                 put(SUM0, t, x, fields[FIRST][t, x + 1] + running)
 
-    phase(up_one, SUM0, functools.partial(send_last, P_SUM0))
+    phase(up_one, SUM0, functools.partial(send_last, P_SUM0), awaited=P_FIX1)
     wait_faces(SUM0)
     wait_last(P_SUM0)
 
@@ -449,13 +475,13 @@
     out_two.start()
 
     for i in range(FIELDS):
-        if i == PAIR or i == (ERR3 if n_tm == 2 else PART):
+        if i in ((PAIR, PAIR2, ERR3, FIX2) if n_tm == 2 else (PART, PAIR, PART2, PAIR2)):
             continue
         for side in (XLO, XHI, YLO, YHI):
             @pl.when(has[side])
             def _(i=i, side=side):
                 face_copy(i, side).wait_send()
-                if i == PART:
+                if i in (PART, PART2):
                     face_copy(i, side, True).wait_send()
 
     @pl.when(tm < n_tm - 1)
@@ -482,7 +508,7 @@
 
     def per_device(heat_source, conductivity, initial_iterate):
         steps, nx, ny, nz = heat_source.shape
-        depth = (1, steps, steps, steps // 2, 1, 1, 1, steps // 2, steps, steps, 1, 1)
+        depth = (1, steps, steps, steps // 2, 1, 1, 1, steps // 2, steps, steps, 1, 1, 1, 1)
         scratch = [pltpu.VMEM((d, nx + 2, ny, nz), f32) for d in depth]
         scratch += [pltpu.VMEM((2, d, nx, nz), f32) for d in depth] * 2
         cells = (nx, ny, nz)

time: 42.9 us -> 41.4 us (0.965)
  Pallas kernels: 39.1 us -> 37.3 us
    pallas_call x1, Pallas kernels: 39.1 us -> 37.3 us  [per_device(): pl.pallas_call(functools.partial(kernel, n_tm, n_sx, n_sy), out_shape=(fi...]
where the time goes in v4:
time: 41.4 us; the launch traced here: 40.6 us
  Pallas kernels  37.3 us (90%)
  local copies, waits for them, and re-layouts  2.72 us (7%)
  between operations  0.65 us (2%)
    pallas_call x1, Pallas kernels, per_device(): pl.pallas_call(functools.partial(kernel, n_tm, n_sx, n_sy), out_shape=(fi...  37.3 us
    unnamed x4, local copies, waits for them, and re-layouts  2.72 us

profile of v4, /device:TPU:0, one launch (start us, length us, event | category | flops | bytes accessed | tf_op | source)
XLA Modules:
  0.0 40.6 jit_solution(9203452207875799012)
XLA Ops:
  0.6 37.3 %vcycle.1 = (f32[4,16,16,128]{3,2,1,0:T(8,128)}, f32[4,16,16,128]{3,2,1,0:T(8,128)}) custom-call(f32[4,16,16,128]{3,2,1,0:T(8,128)} %hs_hbm.1, f32[16,16,128]{2,1,0:T(8,128)} %k_hbm.1, f32[4,16,16,128]{3,2,1,0:T(8,128)} %in_hbm.1), custom_call_target="tpu_custom_call" | custom-call | tf_op jit(solution)/shard_map/vcycle/pallas_call | solution.py:534
  37.9 0.0 copy-start
  37.9 1.9 %copy.7 = f32[4,16,16,128]{3,2,1,0:T(8,128)} copy(f32[4,16,16,128]{3,2,1,0:T(8,128)} %get-tuple-element.4) | data formatting | bytes 1048576
  39.9 0.0 copy-done
  39.9 0.8 %copy.8 = f32[4,16,16,128]{3,2,1,0:T(8,128)} copy(f32[4,16,16,128]{3,2,1,0:T(8,128)S(1)} %copy-done) | data formatting | bytes 1048576
Async XLA Ops:
  37.9 1.9 %copy-start = (f32[4,16,16,128]{3,2,1,0:T(8,128)S(1)}, f32[4,16,16,128]{3,2,1,0:T(8,128)}, u32[]{:S(2)}) copy-start(f32[4,16,16,128]{3,2,1,0:T(8,128)} %get-tuple-element.5) | copy-start | bytes 1572868
